TPU v7x, 128 devices: a whole 4x4x4 slice. The times are simulated.
128 devices in a mesh: vox: 16 (over y, x), dir: 8 (over z, core).
Axes of the slice: x: 4, y: 4, z: 4, core: 2. Of those that a mesh axis runs over, the one named last changes fastest.
Arguments:
- signal: bfloat16 [1200, 262144], P('dir', 'vox'), may hold values from -6 to 6
- response: bfloat16 [153, 1200], replicated, may hold values from -0.1875 to 0.1875
- sphere_basis: bfloat16 [1200, 153], replicated, may hold values from -0.5 to 0.5
- initial: float32 [153, 262144], P(None, ('vox', 'dir')), may hold values from -6 to 6
- similarity: bfloat16 [2048, 27, 128, 128], P(('vox', 'dir')), may hold values from 0.0009994507 to 1
- neighbour_count: int32 [2048], P(('vox', 'dir')), may hold values from 1 to 27
- neighbour_index: int32 [2048, 27], P(('vox', 'dir')), may hold values from 0 to 63, as said below
- fetch_list: int32 [128, 16, 3], P(('vox', 'dir')), may hold values from 0 to 15
Outputs:
- coefficients: float32 [153, 262144], P(None, ('vox', 'dir'))
Inputs may be any that keep to these rules, and one draw needn't show every extreme that they name: `neighbour_index`: the 27 entries of one row are distinct.
All inputs are finite; a program needn't handle non-finite values.
Results may differ from a plain program's by a relative error of at most 0.00033.
Values may be sent and summed in bfloat16 or wider, within the bound.
No kernel may reach another device: no remote copies, remote signals or barrier semaphores. Data moves between devices by JAX's collectives and lax.ppermute only.
A program may use at most 128 MiB of HBM per device.

v0:
```python
import jax
import jax.numpy as jnp
from jax import lax
from jax.sharding import PartitionSpec as P

ITERS = 3


step_size = 0.2
smooth_weight = 2.0
penalty_weight = 0.1
sparsity = 0.25


def local(
    signal,
    response,
    sphere_basis,
    initial,
    similarity,
    neighbour_count,
    neighbour_index,
    fetch_list,
):
    coef_count = initial.shape[0]
    local_voxels = initial.shape[1]
    rows_here = similarity.shape[0]
    slot_count = similarity.shape[1]
    block_span = similarity.shape[2]
    peer_count = lax.axis_size("vox")
    grouped = lax.all_to_all(signal, "dir", split_axis=1, concat_axis=0, tiled=True)
    fitted = jnp.dot(response, grouped, preferred_element_type=jnp.float32)
    gram_matrix = lax.dot_general(
        response, response, (((1,), (1,)), ((), ())), preferred_element_type=jnp.float32
    )
    live_slot = jnp.arange(slot_count, dtype=jnp.int32)[None, :] < neighbour_count[:, None]
    row_sums = jnp.sum(similarity, axis=3, dtype=jnp.float32)
    degree = jnp.sum(jnp.where(live_slot[:, :, None], row_sums, 0.0), axis=1).reshape(
        1, local_voxels
    )
    masked = jnp.where(live_slot[:, :, None, None], similarity, jnp.zeros((), similarity.dtype))
    wanted = fetch_list.reshape(peer_count, -1)
    coeffs = initial
    threshold = step_size * sparsity
    for iteration in range(ITERS):
        rounded = coeffs.astype(jnp.bfloat16)
        own_blocks = rounded.reshape(coef_count, rows_here, block_span).transpose(1, 0, 2)
        everything = lax.all_gather(own_blocks, "vox", axis=0, tiled=True)
        flat_index = (
            jnp.arange(peer_count, dtype=jnp.int32)[:, None] * rows_here + wanted
        ).reshape(-1)
        fetched = everything[flat_index]
        candidates = jnp.concatenate([own_blocks, fetched], axis=0)
        nearby = candidates[neighbour_index]
        graph_term = jnp.einsum(
            "rmab,rmkb->kra", masked, nearby, preferred_element_type=jnp.float32
        ).reshape(coef_count, local_voxels)
        amplitude = jnp.dot(sphere_basis, rounded, preferred_element_type=jnp.float32)
        negative = jnp.minimum(amplitude, 0.0).astype(jnp.bfloat16)
        pulled = lax.dot_general(
            sphere_basis, negative, (((0,), (0,)), ((), ())), preferred_element_type=jnp.float32
        )
        fidelity = jnp.dot(
            gram_matrix, coeffs, precision=lax.Precision.HIGHEST, preferred_element_type=jnp.float32
        )
        gradient = (
            fidelity
            - fitted
            + smooth_weight * (coeffs - graph_term / degree)
            + penalty_weight * pulled
        )
        stepped = coeffs - step_size * gradient
        coeffs = stepped - jnp.clip(stepped, -threshold, threshold)
    return coeffs


def solution(mesh):
    in_specs = (
        P("dir", "vox"),
        P(),
        P(),
        P(None, ("vox", "dir")),
        P(("vox", "dir"), None, None, None),
        P(("vox", "dir")),
        P(("vox", "dir"), None),
        P(("vox", "dir"), None, None),
    )
    out_specs = P(None, ("vox", "dir"))
    return jax.shard_map(local, mesh=mesh, in_specs=in_specs, out_specs=out_specs, check_vma=False)
```

profile of v0, /device:TPU:96, one launch (start us, length us, event | category | flops | bytes accessed | tf_op | source)
XLA Modules:
  0.0 445.3 jit_solution(7337765231145608006)
XLA Ops:
  6.5 1.4 convert_element_type.23
  8.1 1.0 fusion.33
  9.2 6.3 %copy.82 = bf16[19,8,8,2048]{3,2,1,0:T(8,128)(2,1)S(1)} copy(bf16[19,8,8,2048]{3,1,2,0:T(8,128)(2,1)} %bitcast.93) | data formatting | bytes 9961472
  15.5 0.8 slice.12
  16.2 5.0 %copy.60 = bf16[150,8,2048]{2,0,1:T(8,128)(2,1)} copy(bf16[150,8,2048]{2,1,0:T(8,128)(2,1)S(1)} %slice.12) | data formatting | bytes 9830400 | tf_op jit(solution)/shard_map/all_to_all | solution.py:31
  21.2 4.7 %all-to-all-start = ((bf16[150,8,2048]{2,0,1:T(8,128)(2,1)}), bf16[150,8,2048]{2,0,1:T(8,128)(2,1)}, u32[]{:S(2)}, u32[]{:S(2)}) async-start(bf16[150,8,2048]{2,0,1:T(8,128)(2,1)} %copy.60), calls=%async_computation | async-start | bytes 9961472 | tf_op jit(solution)/shard_map/all_to_all | solution.py:31
  25.9 0.5 all-gather.6.cloned.1.call-start
  26.8 1.0 copy.94
  28.0 9.1 %convert_reduce_fusion = f32[16,27,128]{2,1,0:T(8,128)S(1)} fusion(bf16[16,27,128,128]{3,2,1,0:T(8,128)(2,1)} %param.12), kind=kLoop, calls=%fused_computation.6 | loop fusion | flops 14100480 | bytes 14376960 | tf_op jit(solution)/shard_map/reduce_sum | solution.py:37
  37.6 3.4 fusion.8
  41.0 41.0 %all-to-all-done = bf16[150,8,2048]{2,0,1:T(8,128)(2,1)} async-done(((bf16[150,8,2048]{2,0,1:T(8,128)(2,1)}), bf16[150,8,2048]{2,0,1:T(8,128)(2,1)}, u32[]{:S(2)}, u32[]{:S(2)}) %all-to-all-start) | async-done | bytes 4915232 | tf_op jit(solution)/shard_map/all_to_all | solution.py:31
  82.0 4.8 %all_to_all.17 = bf16[1200,2048]{1,0:T(8,128)(2,1)} reshape(bf16[8,150,2048]{2,1,0:T(8,128)(2,1)} %bitcast) | data formatting | bytes 9830400 | tf_op jit(solution)/shard_map/all_to_all | solution.py:31
  86.8 4.6 %fusion.37 = f32[153,2048]{1,0:T(8,128)} fusion(bf16[153,1200]{1,0:T(8,128)(2,1)S(1)} %copy-done.1, bf16[1200,2048]{1,0:T(8,128)(2,1)} %all_to_all.17), kind=kOutput, calls=%fused_computation.73 | convolution fusion | flops 752025600 | bytes 6535776 | tf_op jit(solution)/shard_map/dot_general | solution.py:32
  91.4 6.0 %all-gather.4.cloned.1.call-done = bf16[256,153,128]{2,0,1:T(8,128)(2,1)} async-done(((bf16[16,153,128]{2,0,1:T(8,128)(2,1)}), bf16[256,153,128]{2,0,1:T(8,128)(2,1)}) %all-gather.4.cloned.1.call-update) | async-done | bytes 10027024 | tf_op jit(solution)/shard_map/all_gather | solution.py:48
  97.3 14.4 %copy.64 = bf16[256,153,128]{2,1,0:T(8,128)(2,1)} copy(bf16[256,153,128]{2,0,1:T(8,128)(2,1)} %all-gather.4.cloned.1.call-done) | data formatting | bytes 20054016 | tf_op jit(solution)/shard_map/all_gather | solution.py:48
  111.7 6.1 %gather_fusion = bf16[48,153,128]{2,1,0:T(8,128)(2,1)} fusion(bf16[256,153,128]{2,1,0:T(8,128)(2,1)} %copy.64, s32[1024]{0:T(1024)S(1)} %pad_clamp_fusion.1), kind=kCustom, calls=%fused_computation | custom fusion | bytes 3760320 | tf_op jit(solution)/shard_map/gather | solution.py:52
  117.8 1.9 pad_maximum_fusion
  119.8 14.6 %gather_fusion.1 = bf16[432,153,128]{2,1,0:T(8,128)(2,1)} fusion(bf16[64,153,128]{2,1,0:T(8,128)(2,1)S(1)} %pad_maximum_fusion, s32[1024]{0:T(1024)S(1)} %pad_clamp_fusion), kind=kCustom, calls=%fused_computation.1 | custom fusion | bytes 33842880 | tf_op jit(solution)/shard_map/gather | solution.py:54
  134.3 12.8 %fusion.21 = f32[153,16,128]{2,0,1:T(8,128)S(1)} fusion(bf16[16,27,153,128]{3,2,1,0:T(8,128)(2,1)} %bitcast.88, bf16[16,27,128,128]{3,2,1,0:T(8,128)(2,1)} %param.12, pred[16,27]{1,0:T(8,128)(4,1)S(1)} %iota_compare_fusion), kind=kOutput, calls=%fused_computation.44 | convolution fusion | flops 2172911616 | bytes 32330160 | tf_op jit(solution)/shard_map/rmab,rmkb->kra/dot_general | solution.py:55
  147.1 0.7 copy.65
  148.0 0.5 copy.84
  148.5 0.7 copy-done.2
  150.0 2.8 fusion.34
  152.9 1.0 fusion.32
  154.0 1.0 copy.93
  155.1 3.5 fusion.7
  158.6 81.6 %all-gather.6.cloned.1.call-done = bf16[256,153,128]{2,0,1:T(8,128)(2,1)} async-done(((bf16[16,153,128]{2,0,1:T(8,128)(2,1)}), bf16[256,153,128]{2,0,1:T(8,128)(2,1)}) %all-gather.6.cloned.1.call-update) | async-done | bytes 10027024 | tf_op jit(solution)/shard_map/all_gather | solution.py:48
  240.1 14.4 %copy.69 = bf16[256,153,128]{2,1,0:T(8,128)(2,1)} copy(bf16[256,153,128]{2,0,1:T(8,128)(2,1)} %all-gather.6.cloned.1.call-done) | data formatting | bytes 20054016 | tf_op jit(solution)/shard_map/all_gather | solution.py:48
  254.5 6.1 %gather_fusion.2 = bf16[48,153,128]{2,1,0:T(8,128)(2,1)} fusion(bf16[256,153,128]{2,1,0:T(8,128)(2,1)} %copy.69, s32[1024]{0:T(1024)S(1)} %pad_clamp_fusion.1), kind=kCustom, calls=%fused_computation.2 | custom fusion | bytes 3760320 | tf_op jit(solution)/shard_map/gather | solution.py:52
  260.6 1.9 pad_maximum_fusion.1
  262.5 15.0 %gather_fusion.3 = bf16[432,153,128]{2,1,0:T(8,128)(2,1)} fusion(bf16[64,153,128]{2,1,0:T(8,128)(2,1)S(1)} %pad_maximum_fusion.1, s32[1024]{0:T(1024)S(1)} %pad_clamp_fusion), kind=kCustom, calls=%fused_computation.3 | custom fusion | bytes 33842880 | tf_op jit(solution)/shard_map/gather | solution.py:54
  277.5 12.6 %fusion.22 = f32[153,16,128]{2,0,1:T(8,128)S(1)} fusion(bf16[16,27,153,128]{3,2,1,0:T(8,128)(2,1)} %bitcast.89, bf16[16,27,128,128]{3,2,1,0:T(8,128)(2,1)} %param.12, pred[16,27]{1,0:T(8,128)(4,1)S(1)} %iota_compare_fusion), kind=kOutput, calls=%fused_computation.45 | convolution fusion | flops 2172911616 | bytes 32330160 | tf_op jit(solution)/shard_map/rmab,rmkb->kra/dot_general | solution.py:55
  290.2 0.7 copy.70
  291.0 0.5 copy.86
  291.5 0.7 copy-done.3
  293.0 2.8 fusion.35
  295.9 1.0 fusion.31
  297.0 1.0 copy.92
  298.0 3.5 fusion.6
  301.5 81.6 %all-gather.8.cloned.1.call-done = bf16[256,153,128]{2,0,1:T(8,128)(2,1)} async-done(((bf16[16,153,128]{2,0,1:T(8,128)(2,1)}), bf16[256,153,128]{2,0,1:T(8,128)(2,1)}) %all-gather.8.cloned.1.call-update) | async-done | bytes 10027024 | tf_op jit(solution)/shard_map/all_gather | solution.py:48
  383.1 14.5 %copy.73 = bf16[256,153,128]{2,1,0:T(8,128)(2,1)} copy(bf16[256,153,128]{2,0,1:T(8,128)(2,1)} %all-gather.8.cloned.1.call-done) | data formatting | bytes 20054016 | tf_op jit(solution)/shard_map/all_gather | solution.py:48
  397.7 6.1 %gather_fusion.4 = bf16[48,153,128]{2,1,0:T(8,128)(2,1)} fusion(bf16[256,153,128]{2,1,0:T(8,128)(2,1)} %copy.73, s32[1024]{0:T(1024)S(1)} %pad_clamp_fusion.1), kind=kCustom, calls=%fused_computation.4 | custom fusion | bytes 3760320 | tf_op jit(solution)/shard_map/gather | solution.py:52
  403.8 1.9 pad_maximum_fusion.2
  405.7 14.6 %gather_fusion.5 = bf16[432,153,128]{2,1,0:T(8,128)(2,1)} fusion(bf16[64,153,128]{2,1,0:T(8,128)(2,1)S(1)} %pad_maximum_fusion.2, s32[1024]{0:T(1024)S(1)} %pad_clamp_fusion), kind=kCustom, calls=%fused_computation.5 | custom fusion | bytes 33842880 | tf_op jit(solution)/shard_map/gather | solution.py:54
  420.3 12.6 %fusion.23 = f32[153,16,128]{2,0,1:T(8,128)S(1)} fusion(bf16[16,27,153,128]{3,2,1,0:T(8,128)(2,1)} %bitcast.87, bf16[16,27,128,128]{3,2,1,0:T(8,128)(2,1)} %param.12, pred[16,27]{1,0:T(8,128)(4,1)S(1)} %iota_compare_fusion), kind=kOutput, calls=%fused_computation.46 | convolution fusion | flops 2172911616 | bytes 32330160 | tf_op jit(solution)/shard_map/rmab,rmkb->kra/dot_general | solution.py:55
  432.9 0.7 copy.74
  434.3 0.7 copy-done.4
  435.8 2.8 clamp_subtract_fusion
  (50 shorter events, 4.6 us)
Async XLA Ops:
  6.5 31.0 %copy-start = (bf16[1200,153]{0,1:T(8,128)(2,1)S(1)}, bf16[1200,153]{0,1:T(8,128)(2,1)}, u32[]{:S(2)}) copy-start(bf16[1200,153]{0,1:T(8,128)(2,1)} %param.10) | copy-start | bytes 1101604
  6.5 90.8 %all-gather.4.cloned.1.call-start = ((), (), s32[]{:S(2)}) async-start(), calls=%async_computation.1 | async-start | bytes 10653696 | tf_op jit(solution)/shard_map/all_gather | solution.py:48
  21.2 5.4 %copy-start.7 = (s32[1,16,3]{1,0,2:T(1,128)S(1)}, s32[1,16,3]{1,0,2:T(1,128)}, u32[]{:S(2)}) copy-start(s32[1,16,3]{1,0,2:T(1,128)} %param.15) | copy-start | bytes 580
  21.2 6.6 %copy-start.6 = (s32[16,27]{1,0:T(8,128)S(1)}, s32[16,27]{1,0:T(8,128)}, u32[]{:S(2)}) copy-start(s32[16,27]{1,0:T(8,128)} %param.14) | copy-start | bytes 5188
  21.2 6.8 %copy-start.8 = (s32[16]{0:T(128)S(1)}, s32[16]{0:T(128)}, u32[]{:S(2)}) copy-start(s32[16]{0:T(128)} %param.13) | copy-start | bytes 196
  21.2 60.8 %all-to-all-start = ((bf16[150,8,2048]{2,0,1:T(8,128)(2,1)}), bf16[150,8,2048]{2,0,1:T(8,128)(2,1)}, u32[]{:S(2)}, u32[]{:S(2)}) async-start(bf16[150,8,2048]{2,0,1:T(8,128)(2,1)} %copy.60), calls=%async_computation | async-start | bytes 9961472 | tf_op jit(solution)/shard_map/all_to_all | solution.py:31
  25.9 214.2 %all-gather.6.cloned.1.call-start = ((), (), s32[]{:S(2)}) async-start(), calls=%async_computation.2 | async-start | bytes 10653696 | tf_op jit(solution)/shard_map/all_gather | solution.py:48
  28.0 9.2 %copy-start.1 = (bf16[153,1200]{1,0:T(8,128)(2,1)S(1)}, bf16[153,1200]{1,0:T(8,128)(2,1)}, u32[]{:S(2)}) copy-start(bf16[153,1200]{1,0:T(8,128)(2,1)} %param.9) | copy-start | bytes 1101604
  147.9 1.3 copy-start.2
  147.9 1.7 copy-start.5
  147.9 2.1 copy-start.11
  154.0 229.2 %all-gather.8.cloned.1.call-start = ((), (), s32[]{:S(2)}) async-start(), calls=%async_computation.3 | async-start | bytes 10653696 | tf_op jit(solution)/shard_map/all_gather | solution.py:48
  290.9 1.3 copy-start.3
  290.9 1.7 copy-start.10
  290.9 2.1 copy-start.12
  433.7 1.3 copy-start.4
  433.7 1.7 copy-start.9
  433.7 2.1 copy-start.13
Sparse Core Ops, SparseCore 0:
  9.5 87.8 all-gather.3
  154.1 85.9 all-gather.5
  297.1 85.9 all-gather.7
where the time goes:
time: 453 us; the launch traced here: 445 us
  waiting for transfers between devices  210 us (46%)
  local copies, waits for them, and re-layouts  138 us (30%)
  matrix products  61.7 us (14%)
  other arithmetic  16.5 us (4%)
  between operations  13.6 us (3%)
  starting transfers between devices  5.25 us (1%)
    all_gather x3, waiting for transfers between devices, local(): everything = lax.all_gather(own_blocks, 'vox', axis=0, tiled=True)  169 us
    gather x3, local copies, waits for them, and re-layouts, local(): nearby = candidates[neighbour_index]  44.1 us
    all_gather x3, local copies, waits for them, and re-layouts, local(): everything = lax.all_gather(own_blocks, 'vox', axis=0, tiled=True)  43.2 us
    all_to_all x1, waiting for transfers between devices, local(): lax.all_to_all(signal, 'dir', split_axis=1, concat_axis=0, tiled=True)  41 us
    dot_general x3, matrix products, local(): jnp.einsum('rmab,rmkb->kra', masked, nearby, preferred_element_type=jnp.f...  38.1 us
    gather x3, local copies, waits for them, and re-layouts, local(): fetched = everything[flat_index]  18.4 us
    unnamed x39, local copies, waits for them, and re-layouts  13 us
    all_to_all x3, local copies, waits for them, and re-layouts, local(): lax.all_to_all(signal, 'dir', split_axis=1, concat_axis=0, tiled=True)  10.5 us
  transfers between devices with their start and end apart: 4, of which 4 were waited for; matrix products, arithmetic and copies ran while one was open for 9% of the time, Pallas kernels for 0%

commit v1 on v0

v1 whole, which is shorter than its diff:
```python
import jax
import jax.numpy as jnp
from jax import lax
from jax.experimental import pallas as pl
from jax.experimental.pallas import tpu as pltpu
from jax.sharding import PartitionSpec as P

ITERS = 3
STEP = 0.2
SMOOTH = 2.0
PENALTY = 0.1
THRESHOLD = 0.2 * 0.25
KP = 160
CHUNKS = (160,)
BS = 128
UNROLL = 8
AHEAD = 4
RING = 6
F32 = jnp.float32
BF16 = jnp.bfloat16
SM = pl.BlockSpec(memory_space=pltpu.SMEM)
HBM = pl.BlockSpec(memory_space=pltpu.HBM)


def params(mib=56):
    return pltpu.CompilerParams(vmem_limit_bytes=mib << 20)


def cost(flops, moved):
    return pl.CostEstimate(flops=int(flops), bytes_accessed=int(moved), transcendentals=0)


def shape(dims, kind):
    return jax.ShapeDtypeStruct(dims, kind)


def shrink(x):
    return x - jnp.clip(x, -THRESHOLD, THRESHOLD)


def partial_fit(signal, weights, parts):
    dirs, wide = signal.shape
    rows = weights.shape[0]
    span = wide // parts

    def body(signal_ref, weights_ref, out_ref):
        out_ref[0] = jnp.dot(weights_ref[...], signal_ref[...], preferred_element_type=F32)

    return pl.pallas_call(
        body,
        grid=(parts,),
        in_specs=[
            pl.BlockSpec((dirs, span), lambda i: (0, i)),
            pl.BlockSpec((rows, dirs), lambda i: (0, 0)),
        ],
        out_specs=pl.BlockSpec((1, rows, span), lambda i: (i, 0, 0)),
        out_shape=shape((parts, rows, span), F32),
        compiler_params=params(),
        cost_estimate=cost(2 * rows * dirs * wide, 2 * dirs * wide + 4 * rows * wide),
        name="partial_fit",
    )(signal, weights)


def plan_tasks(count, index):
    rows, slots = index.shape
    room = rows * ((slots + 1) // 2 + 1) + UNROLL

    def body(count_ref, index_ref, own_ref, far_ref, steps_ref):
        def row(r, carry):
            n_own, n_far = carry

            def put(ref, n, held, m, c, zero):
                first = r + 32 * m + 1024 * m + 32768 * c + 4194304 * zero
                whole = held + 1024 * (m - ((held // 32) % 32)) + 4194304 * (c - zero)
                fresh = held < 0
                at = jnp.where(fresh, n, n - 1)
                ref[at] = jnp.where(fresh, first, whole)
                return jnp.where(fresh, n + 1, n), jnp.where(fresh, first, -1)

            def slot(m, inner):
                n_own, n_far, h_own, h_far = inner
                c = index_ref[r, m]
                near = c < rows

                def yes():
                    n, h = put(own_ref, n_own, h_own, m, c, rows)
                    return n, n_far, h, h_far

                def no():
                    n, h = put(far_ref, n_far, h_far, m, c - rows, 48)
                    return n_own, n, h_own, h

                return lax.cond(near, yes, no)

            none = jnp.int32(-1)
            n_own, n_far, _, _ = lax.fori_loop(
                0, count_ref[r], slot, (n_own, n_far, none, none)
            )
            return n_own, n_far

        zero = jnp.int32(0)
        n_own, n_far = lax.fori_loop(0, rows, row, (zero, zero))
        for i in range(UNROLL):
            own_ref[n_own + i] = rows + 32768 * rows + 4194304 * rows
            far_ref[n_far + i] = rows + 32768 * 48 + 4194304 * 48
        steps_ref[0] = (n_own + UNROLL - 1) // UNROLL
        steps_ref[1] = (n_far + UNROLL - 1) // UNROLL

    return pl.pallas_call(
        body,
        in_specs=[SM, SM],
        out_specs=[SM, SM, SM],
        out_shape=[shape((room,), jnp.int32), shape((room,), jnp.int32), shape((2,), jnp.int32)],
        compiler_params=params(),
        cost_estimate=cost(1, 10_000_000),
        name="plan_tasks",
    )(count, index)


def send_blocks(want_ref, own, send_ref, sem):
    peers, cap = want_ref.shape
    for p in range(peers):
        for q in range(cap):
            pltpu.make_async_copy(own.at[want_ref[p, q]], send_ref.at[p * cap + q], sem).start()


def wait_all(ref, sem):
    pltpu.make_async_copy(ref, ref, sem).wait()


def first_pack(initial, want):
    rows, wide = initial.shape
    blocks = wide // BS
    peers, cap = want.shape

    def body(want_ref, initial_ref, own_ref, send_ref, held, own, sems):
        load = pltpu.make_async_copy(initial_ref, held, sems.at[0])
        load.start()
        load.wait()
        for r in range(blocks):
            block = held[:, r * BS : (r + 1) * BS]
            block = jnp.concatenate([block, jnp.ones((KP - rows, BS), F32)], axis=0)
            own[r] = block.astype(BF16)
        send_blocks(want_ref, own, send_ref, sems.at[1])
        keep = pltpu.make_async_copy(own, own_ref, sems.at[2])
        keep.start()
        wait_all(send_ref, sems.at[1])
        keep.wait()

    return pl.pallas_call(
        body,
        in_specs=[SM, HBM],
        out_specs=[HBM, HBM],
        out_shape=[shape((blocks, KP, BS), BF16), shape((peers * cap, KP, BS), BF16)],
        scratch_shapes=[
            pltpu.VMEM((rows, wide), F32),
            pltpu.VMEM((blocks, KP, BS), BF16),
            pltpu.SemaphoreType.DMA((3,)),
        ],
        compiler_params=params(),
        cost_estimate=cost(1, 4 * rows * wide + 2 * (blocks + peers * cap) * KP * BS),
        name="first_pack",
    )(want, initial)


def local_terms(pieces, gram, sphere, sphere_t):
    wide = pieces[0].shape[1]
    rows = sum(p.shape[0] for p in pieces)
    ns = sphere.shape[0]
    tile = 512

    def body(*refs):
        ins, (g_ref, s_ref, st_ref), outs = refs[: len(pieces)], refs[len(pieces) :][:3], refs[len(pieces) + 3 :]
        c = jnp.concatenate(
            [r[...] for r in ins] + ([jnp.zeros((KP - rows, tile), F32)] if rows < KP else []), axis=0
        )
        hi = c.astype(BF16)
        lo = (c - hi.astype(F32)).astype(BF16)
        g = g_ref[...]
        gh = g.astype(BF16)
        gl = (g - gh.astype(F32)).astype(BF16)
        fid = jnp.dot(gh, hi, preferred_element_type=F32)
        fid += jnp.dot(gh, lo, preferred_element_type=F32)
        fid += jnp.dot(gl, hi, preferred_element_type=F32)
        amplitude = jnp.dot(s_ref[...], hi, preferred_element_type=F32)
        negative = jnp.minimum(amplitude, 0.0).astype(BF16)
        pulled = jnp.dot(st_ref[...], negative, preferred_element_type=F32)
        value = c - STEP * (fid + SMOOTH * c + PENALTY * pulled)
        at = 0
        for ref, k in zip(outs, CHUNKS):
            ref[...] = value[at : at + k]
            at += k

    def whole(*dims):
        return pl.BlockSpec(dims, lambda i: (0,) * len(dims))

    return pl.pallas_call(
        body,
        grid=(wide // tile,),
        in_specs=[pl.BlockSpec((p.shape[0], tile), lambda i: (0, i)) for p in pieces]
        + [whole(KP, KP), whole(ns, KP), whole(KP, ns)],
        out_specs=[pl.BlockSpec((k, tile), lambda i: (0, i)) for k in CHUNKS],
        out_shape=[shape((k, wide), F32) for k in CHUNKS],
        compiler_params=params(),
        cost_estimate=cost(2 * wide * KP * (3 * KP + 2 * ns), 8 * KP * wide),
        name="local_terms",
    )(*pieces, gram, sphere, sphere_t)


def run_tasks(tasks_ref, steps, blocks_ref, sim_ref, acc_ref, ring, sems, before):
    rows = sim_ref.shape[0]
    nt = (((1,), (1,)), ((), ()))
    wide = 2 * UNROLL

    def fetch(s):
        slot = lax.rem(s, RING)
        for u in range(UNROLL):
            t = tasks_ref[s * UNROLL + u]
            r = jnp.minimum(t & 31, rows - 1)
            for i, m in enumerate(((t >> 5) & 31, (t >> 10) & 31)):
                to = ring.at[slot * wide + (2 * u + i)]
                pltpu.make_async_copy(sim_ref.at[r, m], to, sems.at[slot]).start()

    for s in range(AHEAD):

        @pl.when(s < steps)
        def _():
            fetch(jnp.int32(s))

    before()

    def step(s, carry):
        slot = lax.rem(s, RING)

        @pl.when(s + AHEAD < steps)
        def _():
            fetch(s + AHEAD)

        wait_all(ring.at[pl.ds(slot * wide, wide)], sems.at[slot])
        made = []
        for u in range(UNROLL):
            t = tasks_ref[s * UNROLL + u]
            at = slot * wide + 2 * u
            left = jnp.concatenate([blocks_ref[(t >> 15) & 127], blocks_ref[(t >> 22) & 127]], axis=1)
            right = jnp.concatenate([ring[at], ring[at + 1]], axis=1)
            made.append((t & 31, lax.dot_general(left, right, nt, preferred_element_type=F32)))
        for r, d in made:
            acc_ref[r] = acc_ref[r] + d
        return carry

    lax.fori_loop(0, steps, step, 0)


def graph_call(which, tasks, steps, blocks, similarity, extra, finish, out_shape, scratch, sems, name):
    rows = similarity.shape[0]
    given, k, _ = blocks.shape
    loaded = [x for x in extra if x.dtype != jnp.int32]

    def body(tasks_ref, steps_ref, blocks_ref, sim_ref, *rest):
        extra_refs, rest = rest[: len(extra)], rest[len(extra) :]
        outs, rest = rest[: len(out_shape)], rest[len(out_shape) :]
        held, acc, ring, ring_sems, load_sems, *rest = rest
        buffers, rest = rest[: len(loaded)], rest[len(loaded) :]
        own_scratch, own_sems = rest[: len(scratch)], rest[len(scratch) :]
        first = pltpu.make_async_copy(blocks_ref, held.at[pl.ds(0, given)], load_sems.at[0])
        first.start()
        held[given] = jnp.zeros((k, BS), BF16)
        for r in range(rows + 1):
            acc[r] = jnp.zeros((k, BS), F32)
        loads, ready = [], []
        left = list(buffers)
        for x, ref in zip(extra, extra_refs):
            if x.dtype == jnp.int32:
                ready.append(ref)
                continue
            to = left.pop(0)
            ready.append(to)
            loads.append(pltpu.make_async_copy(ref, to, load_sems.at[len(loads) + 1]))

        def before():
            for load in loads:
                load.start()
            first.wait()

        run_tasks(tasks_ref, steps_ref[which], held, sim_ref, acc, ring, ring_sems, before)
        for load in loads:
            load.wait()
        finish(acc, ready, outs, own_scratch, own_sems[0] if own_sems else None)

    return pl.pallas_call(
        body,
        in_specs=[SM, SM, HBM, HBM] + [SM if x.dtype == jnp.int32 else HBM for x in extra],
        out_specs=[HBM] * len(out_shape),
        out_shape=out_shape,
        scratch_shapes=[
            pltpu.VMEM((given + 1, k, BS), BF16),
            pltpu.VMEM((rows + 1, k, BS), F32),
            pltpu.VMEM((RING * 2 * UNROLL, BS, BS), BF16),
            pltpu.SemaphoreType.DMA((RING,)),
            pltpu.SemaphoreType.DMA((len(loaded) + 1,)),
        ]
        + [pltpu.VMEM(x.shape, x.dtype) for x in loaded]
        + scratch
        + [pltpu.SemaphoreType.DMA((sems,))],
        compiler_params=params(),
        cost_estimate=cost(2 * k * BS * BS * rows * 14, 8_000_000),
        name=name,
    )(tasks, steps, blocks, similarity, *extra)


def first_own(tasks, steps, own, similarity):
    rows = similarity.shape[0]
    k = own.shape[1]

    def finish(acc, extra, outs, scratch, sems):
        out = pltpu.make_async_copy(acc.at[pl.ds(0, rows)], outs[0], sems.at[0])
        out.start()
        out.wait()

    (summed,) = graph_call(
        0, tasks, steps, own, similarity, [], finish, [shape((rows, k, BS), F32)], [], 1, "first_own"
    )
    return summed


def first_far(tasks, steps, recv, similarity, summed, bases):
    rows = similarity.shape[0]
    wide = rows * BS

    def finish(acc, extra, outs, scratch, sems):
        sum_ref, *base_refs = extra
        for r in range(rows):
            at = slice(r * BS, (r + 1) * BS)
            total = acc[r] + sum_ref[r]
            factor = (STEP * SMOOTH) / total[KP - 1 : KP]
            total = total * factor
            low = 0
            for base_ref, to, k in zip(base_refs, scratch, CHUNKS):
                to[:, at] = base_ref[:, at] + total[low : low + k]
                low += k
            scratch[-1][:, at] = jnp.broadcast_to(factor, (8, BS))
        copies = [pltpu.make_async_copy(s, o, sems.at[i]) for i, (s, o) in enumerate(zip(scratch, outs))]
        for copy in copies:
            copy.start()
        for copy in copies:
            copy.wait()

    dims = [(k, wide) for k in CHUNKS] + [(8, wide)]
    *mixed, factor = graph_call(
        1,
        tasks,
        steps,
        recv,
        similarity,
        [summed, *bases],
        finish,
        [shape(d, F32) for d in dims],
        [pltpu.VMEM(d, F32) for d in dims],
        len(dims),
        "first_far",
    )
    return mixed, factor


def next_own(tasks, steps, own, similarity, base, fitted, factor):
    rows = similarity.shape[0]
    wide = rows * BS
    k = own.shape[1]

    def finish(acc, extra, outs, scratch, sems):
        base_ref, fit_ref, factor_ref = extra
        for r in range(rows):
            at = slice(r * BS, (r + 1) * BS)
            scratch[0][:, at] = base_ref[:, at] + STEP * fit_ref[:, at] + acc[r] * factor_ref[0:1, at]
        out = pltpu.make_async_copy(scratch[0], outs[0], sems.at[0])
        out.start()
        out.wait()

    (pre,) = graph_call(
        0,
        tasks,
        steps,
        own,
        similarity,
        [base, fitted, factor],
        finish,
        [shape((k, wide), F32)],
        [pltpu.VMEM((k, wide), F32)],
        1,
        "next_own",
    )
    return pre


def hand_on(values, want_ref, outs, scratch, sems):
    out_ref, own_ref, send_ref = outs
    out, own = scratch
    for r in range(own.shape[0]):
        value = values(r)
        out[:, r * BS : (r + 1) * BS] = value
        own[r] = value.astype(BF16)
    send_blocks(want_ref, own, send_ref, sems.at[0])
    copies = [
        pltpu.make_async_copy(own, own_ref, sems.at[1]),
        pltpu.make_async_copy(out, out_ref, sems.at[2]),
    ]
    for copy in copies:
        copy.start()
    wait_all(send_ref, sems.at[0])
    for copy in copies:
        copy.wait()


def next_far(tasks, steps, recv, similarity, pre, factor, want):
    rows = similarity.shape[0]
    wide = rows * BS
    k = recv.shape[1]

    def finish(acc, extra, outs, scratch, sems):
        pre_ref, factor_ref, want_ref = extra

        def values(r):
            at = slice(r * BS, (r + 1) * BS)
            return shrink(pre_ref[:, at] + acc[r] * factor_ref[0:1, at])

        hand_on(values, want_ref, outs, scratch, sems)

    return graph_call(
        1,
        tasks,
        steps,
        recv,
        similarity,
        [pre, factor, want],
        finish,
        [shape((k, wide), F32), shape((rows, k, BS), BF16), shape(recv.shape, BF16)],
        [pltpu.VMEM((k, wide), F32), pltpu.VMEM((rows, k, BS), BF16)],
        3,
        "next_far",
    )


def last_far(tasks, steps, recv, similarity, pre, factor, above, out_rows):
    rows = similarity.shape[0]
    wide = rows * BS

    def finish(acc, extra, outs, scratch, sems):
        pre_ref, factor_ref, *done = extra
        (out,) = scratch
        low = 0
        for ref in done:
            out[low : low + ref.shape[0], :] = ref[...]
            low += ref.shape[0]
        for r in range(rows):
            at = slice(r * BS, (r + 1) * BS)
            value = shrink(pre_ref[:, at] + acc[r] * factor_ref[0:1, at])
            out[low:out_rows, at] = value[: out_rows - low]
        copy = pltpu.make_async_copy(out, outs[0], sems.at[0])
        copy.start()
        copy.wait()

    (coeffs,) = graph_call(
        1,
        tasks,
        steps,
        recv,
        similarity,
        [pre, factor, *above],
        finish,
        [shape((out_rows, wide), F32)],
        [pltpu.VMEM((out_rows, wide), F32)],
        1,
        "last_far",
    )
    return coeffs


def finish_first(mixed, fitted, want):
    k, wide = mixed.shape
    rows = wide // BS
    peers, cap = want.shape

    def body(want_ref, mixed_ref, fit_ref, out_ref, own_ref, send_ref, mix, fit, out, own, sems):
        loads = [
            pltpu.make_async_copy(mixed_ref, mix, sems.at[3]),
            pltpu.make_async_copy(fit_ref, fit, sems.at[4]),
        ]
        for load in loads:
            load.start()
        for load in loads:
            load.wait()

        def values(r):
            at = slice(r * BS, (r + 1) * BS)
            return shrink(mix[:, at] + STEP * fit[:, at])

        hand_on(values, want_ref, (out_ref, own_ref, send_ref), (out, own), sems)

    return pl.pallas_call(
        body,
        in_specs=[SM, HBM, HBM],
        out_specs=[HBM] * 3,
        out_shape=[
            shape((k, wide), F32),
            shape((rows, k, BS), BF16),
            shape((peers * cap, k, BS), BF16),
        ],
        scratch_shapes=[
            pltpu.VMEM((k, wide), F32),
            pltpu.VMEM((k, wide), F32),
            pltpu.VMEM((k, wide), F32),
            pltpu.VMEM((rows, k, BS), BF16),
            pltpu.SemaphoreType.DMA((5,)),
        ],
        compiler_params=params(),
        cost_estimate=cost(1, 12 * k * wide),
        name="finish_first",
    )(want, mixed, fitted)


def local(
    signal,
    response,
    sphere_basis,
    initial,
    similarity,
    neighbour_count,
    neighbour_index,
    fetch_list,
):
    coef_count = initial.shape[0]
    peers = lax.axis_size("vox")
    parts = lax.axis_size("dir")
    dirs = signal.shape[0]
    pad = KP - coef_count

    response = jnp.pad(response, ((0, pad), (0, 0)))
    mine = lax.dynamic_slice_in_dim(response, lax.axis_index("dir") * dirs, dirs, axis=1)
    fitted = []
    low = 0
    for k in CHUNKS:
        piece = partial_fit(signal, mine[low : low + k], parts)
        low += k
        fitted.append(
            lax.psum_scatter(piece.reshape(parts * k, -1), "dir", scatter_dimension=0, tiled=True)
        )
    want = lax.all_to_all(
        fetch_list.reshape(peers, -1), "vox", split_axis=0, concat_axis=0, tiled=True
    )
    gram = lax.dot_general(response, response, (((1,), (1,)), ((), ())), preferred_element_type=F32)
    sphere = jnp.pad(sphere_basis, ((0, 0), (0, pad)))
    sphere_t = sphere.T

    def exchange(send):
        moved = lax.all_to_all(
            send.reshape(peers, -1, BS), "vox", split_axis=0, concat_axis=0, tiled=True
        )
        return moved.reshape(send.shape)

    near, far, steps = plan_tasks(neighbour_count, neighbour_index)

    own, send = first_pack(initial, want)
    recv = exchange(send)
    base = local_terms([initial], gram, sphere, sphere_t)
    summed = first_own(near, steps, own, similarity)
    mixed, factor = first_far(far, steps, recv, similarity, summed, base)
    state = [finish_first(m, f, want) for m, f in zip(mixed, fitted)]
    for iteration in range(1, ITERS):
        recv = [exchange(send) for _, _, send in state]
        base = local_terms([c for c, _, _ in state], gram, sphere, sphere_t)
        pre = [
            next_own(near, steps, own, similarity, b, f, factor)
            for (_, own, _), b, f in zip(state, base, fitted)
        ]
        if iteration < ITERS - 1:
            state = [
                next_far(far, steps, v, similarity, p, factor, want) for v, p in zip(recv, pre)
            ]
        else:
            above = [
                next_far(far, steps, v, similarity, p, factor, want)[0]
                for v, p in zip(recv[:-1], pre[:-1])
            ]
            coeffs = last_far(far, steps, recv[-1], similarity, pre[-1], factor, above, coef_count)
    return coeffs


def solution(mesh):
    in_specs = (
        P("dir", "vox"),
        P(),
        P(),
        P(None, ("vox", "dir")),
        P(("vox", "dir"), None, None, None),
        P(("vox", "dir")),
        P(("vox", "dir"), None),
        P(("vox", "dir"), None, None),
    )
    out_specs = P(None, ("vox", "dir"))
    return jax.shard_map(local, mesh=mesh, in_specs=in_specs, out_specs=out_specs, check_vma=False)
```

time: 453 us -> 189 us (0.42)
  the two profiles are of different devices: /device:TPU:96 before, /device:TPU:32 now
where the time goes in v1:
time: 189 us; the launch traced here: 187 us
  Pallas kernels  85.2 us (45%)
  waiting for transfers between devices  49.6 us (26%)
  starting transfers between devices  14.6 us (8%)
  blocking collectives  14.4 us (8%)
  between operations  13.5 us (7%)
  local copies, waits for them, and re-layouts  8.98 us (5%)
    all_to_all x3, waiting for transfers between devices, exchange(): lax.all_to_all(send.reshape(peers, -1, BS), 'vox', split_axis=0, concat_a...  48.6 us
    pallas_call x6, Pallas kernels, graph_call(): pl.pallas_call(body, in_specs=[SM, SM, HBM, HBM] + [SM if x.dtype == jnp....  41.3 us
    pallas_call x3, Pallas kernels, local_terms(): pl.pallas_call(body, grid=(wide // tile,), in_specs=[pl.BlockSpec((p.shap...  17.5 us
    all_to_all x3, starting transfers between devices, exchange(): lax.all_to_all(send.reshape(peers, -1, BS), 'vox', split_axis=0, concat_a...  14.6 us
    all_to_all x1, blocking collectives, local(): lax.all_to_all(fetch_list.reshape(peers, -1), 'vox', split_axis=0, concat...  14.4 us
    pallas_call x1, Pallas kernels, plan_tasks(): pl.pallas_call(body, in_specs=[SM, SM], out_specs=[SM, SM, SM], out_shape...  9.17 us
    pallas_call x1, Pallas kernels, partial_fit(): pl.pallas_call(body, grid=(parts,), in_specs=[pl.BlockSpec((dirs, span),...  8.79 us
    unnamed x13, local copies, waits for them, and re-layouts  4.76 us
  transfers between devices with their start and end apart: 4, of which 4 were waited for; matrix products, arithmetic and copies ran while one was open for 2% of the time, Pallas kernels for 28%

profile of v1, /device:TPU:32, one launch (start us, length us, event | category | flops | bytes accessed | tf_op | source)
XLA Modules:
  0.0 187.2 jit_solution(13514981681337924513)
XLA Ops:
  6.5 0.0 reduce-scatter.2.cloned.1.call-start
  6.5 1.6 pad_dynamic-slice_fusion.weights_ref
  8.2 8.8 %partial_fit.1 = f32[8,160,2048]{2,1,0:T(8,128)} custom-call(bf16[150,16384]{1,0:T(8,128)(2,1)} %signal_ref.1, bf16[160,150]{1,0:T(8,128)(2,1)} %pad_dynamic-slice_fusion.weights_ref), custom_call_target="tpu_custom_call" | custom-call | flops 786432000 | bytes 15400960 | tf_op jit(solution)/shard_map/partial_fit/pallas_call | solution.py:49
  17.0 0.0 copy-start.5
  17.0 0.0 reduce-scatter.2.cloned.1.call-update
  17.0 0.7 copy-done.5
  17.6 0.1 copy.23
  17.7 14.4 %all_to_all.26 = s32[16,1,3]{2,1,0:T(1,128)S(1)} all-to-all(s32[16,1,3]{2,1,0:T(1,128)S(1)} %copy.23), channel_id=1, replica_groups=mesh['vox'=16,'dir'=8] {'vox'}, dimensions={0} | all-to-all | bytes 384 | tf_op jit(solution)/shard_map/all_to_all | solution.py:547
  32.1 0.1 copy.24
  32.2 0.7 copy.27.want_ref.rest_2_
  32.9 3.7 %first_pack.1 = (bf16[16,160,128]{2,1,0:T(8,128)(2,1)}, bf16[48,160,128]{2,1,0:T(8,128)(2,1)}) custom-call(s32[16,3]{1,0:T(8,128)} %copy.27.want_ref.rest_2_, f32[153,2048]{1,0:T(8,128)} %refs_0_.1), custom_call_target="tpu_custom_call" | custom-call | flops 1 | bytes 3874816 | tf_op jit(solution)/shard_map/first_pack/pallas_call | solution.py:150
  36.5 0.0 copy-start.3
  36.6 3.9 %all-to-all-start.1 = ((bf16[16,480,128]{2,1,0:T(8,128)(2,1)}), bf16[16,480,128]{2,1,0:T(8,128)(2,1)S(1)}, u32[]{:S(2)}, u32[]{:S(2)}) async-start(bf16[16,480,128]{2,1,0:T(8,128)(2,1)} %bitcast.15), calls=%async_computation.1 | async-start | bytes 3932160 | tf_op jit(solution)/shard_map/all_to_all | solution.py:555
  40.4 0.0 copy-start.4
  40.4 9.2 %plan_tasks.1 = (s32[248]{0:T(256)}, s32[248]{0:T(256)}, s32[2]{0:T(128)}) custom-call(s32[16]{0:T(128)} %count_ref.1, s32[16,27]{1,0:T(8,128)} %index_ref.1), custom_call_target="tpu_custom_call" | custom-call | flops 1 | bytes 10000000 | tf_op jit(solution)/shard_map/plan_tasks/pallas_call | solution.py:109
  49.6 0.0 copy-done.3
  49.6 0.2 copy.31
  49.9 0.9 pad.9.clone.refs_2_
  50.8 0.0 copy-done.4
  50.8 1.0 fusion.refs_1_
  51.8 0.8 pad_bitcast_fusion.refs_3_
  52.6 5.9 %local_terms.3.rest_1_ = f32[160,2048]{1,0:T(8,128)} custom-call(f32[153,2048]{1,0:T(8,128)} %refs_0_.1, f32[160,160]{1,0:T(8,128)} %fusion.refs_1_, bf16[1200,160]{1,0:T(8,128)(2,1)} %pad.9.clone.refs_2_, bf16[160,1200]{1,0:T(8,128)(2,1)} %pad_bitcast_fusion.refs_3_), custom_call_target="tpu_custom_call" | custom-call | flops 1887436800 | bytes 2621440 | tf_op jit(solution)/shard_map/local_terms/pallas_call | solution.py:197
  58.4 4.6 %first_own.1.rest_0_ = f32[16,160,128]{2,1,0:T(8,128)} custom-call(s32[248]{0:T(256)} %get-tuple-element.21.tasks_ref, s32[2]{0:T(128)} %get-tuple-element.19.steps_ref, bf16[16,160,128]{2,1,0:T(8,128)(2,1)} %get-tuple-element.22.blocks_ref, bf16[16,27,128,128]{3,2,1,0:T(8,128)(2,1)} %sim_ref.11), custom_call_target="tpu_custom_call" | custom-call | flops 1174405120 | bytes 8000000 | tf_op jit(solution)/shard_map/first_own/pallas_call | solution.py:290
  63.0 5.1 %all-to-all-done.1 = bf16[16,480,128]{2,1,0:T(8,128)(2,1)S(1)} async-done(((bf16[16,480,128]{2,1,0:T(8,128)(2,1)}), bf16[16,480,128]{2,1,0:T(8,128)(2,1)S(1)}, u32[]{:S(2)}, u32[]{:S(2)}) %all-to-all-start.1) | async-done | bytes 1966112 | tf_op jit(solution)/shard_map/all_to_all | solution.py:555
  68.1 0.0 copy-start.1
  68.1 1.3 copy-done.1
  69.4 8.7 %first_far.1 = (f32[160,2048]{1,0:T(8,128)}, f32[8,2048]{1,0:T(8,128)}) custom-call(s32[248]{0:T(256)} %get-tuple-element.18.tasks_ref, s32[2]{0:T(128)} %get-tuple-element.19.steps_ref, bf16[48,160,128]{2,1,0:T(8,128)(2,1)} %bitcast.13, bf16[16,27,128,128]{3,2,1,0:T(8,128)(2,1)} %sim_ref.11, f32[16,160,128]{2,1,0:T(8,128)} %first_own.1.rest_0_, ...), custom_call_target="tpu_custom_call" | custom-call | flops 1174405120 | bytes 8000000 | tf_op jit(solution)/shard_map/first_far/pallas_call | solution.py:290
  78.1 1.0 reduce-scatter.2.cloned.1.call-done.fit_ref.rest_1_
  79.1 4.8 %finish_first.1 = (f32[160,2048]{1,0:T(8,128)}, bf16[16,160,128]{2,1,0:T(8,128)(2,1)}, bf16[48,160,128]{2,1,0:T(8,128)(2,1)}) custom-call(s32[16,3]{1,0:T(8,128)} %copy.27.want_ref.rest_2_, f32[160,2048]{1,0:T(8,128)} %get-tuple-element.23.mixed_ref, f32[160,2048]{1,0:T(8,128)} %reduce-scatter.2.cloned.1.call-done.fit_ref.rest_1_), custom_call_target="tpu_custom_call" | custom-call | flops 1 | bytes 3932160 | tf_op jit(solution)/shard_map/finish_first/pallas_call | solution.py:499
  83.8 7.0 %all-to-all-start.2 = ((bf16[16,480,128]{2,1,0:T(8,128)(2,1)}), bf16[16,480,128]{2,1,0:T(8,128)(2,1)S(1)}, u32[]{:S(2)}, u32[]{:S(2)}) async-start(bf16[16,480,128]{2,1,0:T(8,128)(2,1)} %bitcast.17), calls=%async_computation.3 | async-start | bytes 3932160 | tf_op jit(solution)/shard_map/all_to_all | solution.py:555
  90.9 5.8 %local_terms.4.rest_0_ = f32[160,2048]{1,0:T(8,128)} custom-call(f32[160,2048]{1,0:T(8,128)} %get-tuple-element.26.refs_0_, f32[160,160]{1,0:T(8,128)} %fusion.refs_1_, bf16[1200,160]{1,0:T(8,128)(2,1)} %pad.9.clone.refs_2_, bf16[160,1200]{1,0:T(8,128)(2,1)} %pad_bitcast_fusion.refs_3_), custom_call_target="tpu_custom_call" | custom-call | flops 1887436800 | bytes 2621440 | tf_op jit(solution)/shard_map/local_terms/pallas_call | solution.py:197
  96.7 4.9 %next_own.2.rest_0_ = f32[160,2048]{1,0:T(8,128)} custom-call(s32[248]{0:T(256)} %get-tuple-element.21.tasks_ref, s32[2]{0:T(128)} %get-tuple-element.19.steps_ref, bf16[16,160,128]{2,1,0:T(8,128)(2,1)} %get-tuple-element.25.blocks_ref, bf16[16,27,128,128]{3,2,1,0:T(8,128)(2,1)} %sim_ref.11, f32[160,2048]{1,0:T(8,128)} %local_terms.4.rest_0_, ...), custom_call_target="tpu_custom_call" | custom-call | flops 1174405120 | bytes 8000000 | tf_op jit(solution)/shard_map/next_own/pallas_call | solution.py:290
  101.7 22.7 %all-to-all-done.2 = bf16[16,480,128]{2,1,0:T(8,128)(2,1)S(1)} async-done(((bf16[16,480,128]{2,1,0:T(8,128)(2,1)}), bf16[16,480,128]{2,1,0:T(8,128)(2,1)S(1)}, u32[]{:S(2)}, u32[]{:S(2)}) %all-to-all-start.2) | async-done | bytes 1966112 | tf_op jit(solution)/shard_map/all_to_all | solution.py:555
  124.4 0.0 copy-start
  124.4 1.3 copy-done
  125.7 9.7 %next_far.1 = (f32[160,2048]{1,0:T(8,128)}, bf16[16,160,128]{2,1,0:T(8,128)(2,1)}, bf16[48,160,128]{2,1,0:T(8,128)(2,1)}) custom-call(s32[248]{0:T(256)} %get-tuple-element.18.tasks_ref, s32[2]{0:T(128)} %get-tuple-element.19.steps_ref, bf16[48,160,128]{2,1,0:T(8,128)(2,1)} %bitcast.12, bf16[16,27,128,128]{3,2,1,0:T(8,128)(2,1)} %sim_ref.11, ...), custom_call_target="tpu_custom_call" | custom-call | flops 1174405120 | bytes 8000000 | tf_op jit(solution)/shard_map/next_far/pallas_call | solution.py:290
  135.4 3.7 %all-to-all-start.3 = ((bf16[16,480,128]{2,1,0:T(8,128)(2,1)}), bf16[16,480,128]{2,1,0:T(8,128)(2,1)S(1)}, u32[]{:S(2)}, u32[]{:S(2)}) async-start(bf16[16,480,128]{2,1,0:T(8,128)(2,1)} %bitcast.16), calls=%async_computation.4 | async-start | bytes 3932160 | tf_op jit(solution)/shard_map/all_to_all | solution.py:555
  139.1 5.8 %local_terms.5.rest_0_ = f32[160,2048]{1,0:T(8,128)} custom-call(f32[160,2048]{1,0:T(8,128)} %get-tuple-element.30.refs_0_, f32[160,160]{1,0:T(8,128)} %fusion.refs_1_, bf16[1200,160]{1,0:T(8,128)(2,1)} %pad.9.clone.refs_2_, bf16[160,1200]{1,0:T(8,128)(2,1)} %pad_bitcast_fusion.refs_3_), custom_call_target="tpu_custom_call" | custom-call | flops 1887436800 | bytes 2621440 | tf_op jit(solution)/shard_map/local_terms/pallas_call | solution.py:197
  144.9 4.8 %next_own.3.rest_0_ = f32[160,2048]{1,0:T(8,128)} custom-call(s32[248]{0:T(256)} %get-tuple-element.21.tasks_ref, s32[2]{0:T(128)} %get-tuple-element.19.steps_ref, bf16[16,160,128]{2,1,0:T(8,128)(2,1)} %get-tuple-element.29.blocks_ref, bf16[16,27,128,128]{3,2,1,0:T(8,128)(2,1)} %sim_ref.11, f32[160,2048]{1,0:T(8,128)} %local_terms.5.rest_0_, ...), custom_call_target="tpu_custom_call" | custom-call | flops 1174405120 | bytes 8000000 | tf_op jit(solution)/shard_map/next_own/pallas_call | solution.py:290
  149.7 20.7 %all-to-all-done.3 = bf16[16,480,128]{2,1,0:T(8,128)(2,1)S(1)} async-done(((bf16[16,480,128]{2,1,0:T(8,128)(2,1)}), bf16[16,480,128]{2,1,0:T(8,128)(2,1)S(1)}, u32[]{:S(2)}, u32[]{:S(2)}) %all-to-all-start.3) | async-done | bytes 1966112 | tf_op jit(solution)/shard_map/all_to_all | solution.py:555
  170.5 0.0 copy-start.2
  170.5 1.3 copy-done.2
  171.8 8.6 %last_far.1 = f32[153,2048]{1,0:T(8,128)} custom-call(s32[248]{0:T(256)} %get-tuple-element.18.tasks_ref, s32[2]{0:T(128)} %get-tuple-element.19.steps_ref, bf16[48,160,128]{2,1,0:T(8,128)(2,1)} %bitcast.14, bf16[16,27,128,128]{3,2,1,0:T(8,128)(2,1)} %sim_ref.11, f32[160,2048]{1,0:T(8,128)} %next_own.3.rest_0_, f32[8,2048]{1,0:T(8,128)} %get-tuple-element.27.rest_2_.rest_1_), custom_call_target="tpu_custom_call" | custom-call | flops 1174405120 | bytes 8000000 | tf_op jit(solution)/shard_map/last_far/pallas_call | solution.py:290
Async XLA Ops:
  6.5 72.6 %reduce-scatter.2.cloned.1.call-start = ((), (), s32[]{:S(2)}) async-start(), calls=%async_computation.5 | async-start | bytes 11796480 | tf_op jit(solution)/shard_map/reduce_scatter | solution.py:545
  17.0 0.7 copy-start.5
  36.5 13.1 %copy-start.3 = (bf16[1200,153]{0,1:T(8,128)(2,1)S(1)}, bf16[1200,153]{0,1:T(8,128)(2,1)}, u32[]{:S(2)}) copy-start(bf16[1200,153]{0,1:T(8,128)(2,1)} %param.10) | copy-start | bytes 1101604
  36.6 31.6 %all-to-all-start.1 = ((bf16[16,480,128]{2,1,0:T(8,128)(2,1)}), bf16[16,480,128]{2,1,0:T(8,128)(2,1)S(1)}, u32[]{:S(2)}, u32[]{:S(2)}) async-start(bf16[16,480,128]{2,1,0:T(8,128)(2,1)} %bitcast.15), calls=%async_computation.1 | async-start | bytes 3932160 | tf_op jit(solution)/shard_map/all_to_all | solution.py:555
  40.4 10.4 %copy-start.4 = (bf16[153,1200]{1,0:T(8,128)(2,1)S(1)}, bf16[153,1200]{1,0:T(8,128)(2,1)}, u32[]{:S(2)}) copy-start(bf16[153,1200]{1,0:T(8,128)(2,1)} %param.9) | copy-start | bytes 1101604
  68.1 1.3 copy-start.1
  83.8 40.6 %all-to-all-start.2 = ((bf16[16,480,128]{2,1,0:T(8,128)(2,1)}), bf16[16,480,128]{2,1,0:T(8,128)(2,1)S(1)}, u32[]{:S(2)}, u32[]{:S(2)}) async-start(bf16[16,480,128]{2,1,0:T(8,128)(2,1)} %bitcast.17), calls=%async_computation.3 | async-start | bytes 3932160 | tf_op jit(solution)/shard_map/all_to_all | solution.py:555
  124.4 1.3 copy-start
  135.4 35.1 %all-to-all-start.3 = ((bf16[16,480,128]{2,1,0:T(8,128)(2,1)}), bf16[16,480,128]{2,1,0:T(8,128)(2,1)S(1)}, u32[]{:S(2)}, u32[]{:S(2)}) async-start(bf16[16,480,128]{2,1,0:T(8,128)(2,1)} %bitcast.16), calls=%async_computation.4 | async-start | bytes 3932160 | tf_op jit(solution)/shard_map/all_to_all | solution.py:555
  170.5 1.3 copy-start.2
Sparse Core Ops, SparseCore 0:
  17.1 61.9 reduce-scatter.1

commit v2 on v1

v2 whole, which is shorter than its diff:
```python
import jax
import jax.numpy as jnp
from jax import lax
from jax.experimental import pallas as pl
from jax.experimental.pallas import tpu as pltpu
from jax.sharding import PartitionSpec as P

ITERS = 3
STEP = 0.2
SMOOTH = 2.0
PENALTY = 0.1
THRESHOLD = 0.2 * 0.25
KP = 160
CHUNKS = (160,)
BS = 128
UNROLL = 8
AHEAD = 4
RING = 6
F32 = jnp.float32
BF16 = jnp.bfloat16
SM = pl.BlockSpec(memory_space=pltpu.SMEM)
HBM = pl.BlockSpec(memory_space=pltpu.HBM)
VM = pl.BlockSpec(memory_space=pltpu.VMEM)
ANY = pl.BlockSpec(memory_space=pl.ANY)


def params(mib=52):
    return pltpu.CompilerParams(vmem_limit_bytes=mib << 20)


def cost(flops, moved):
    return pl.CostEstimate(flops=int(flops), bytes_accessed=int(moved), transcendentals=0)


def shape(dims, kind):
    return jax.ShapeDtypeStruct(dims, kind)


def shrink(x):
    return x - jnp.clip(x, -THRESHOLD, THRESHOLD)


def partial_fit(place, signal, response, parts):
    dirs, wide = signal.shape
    rows = response.shape[0]
    span = wide // parts
    blocks = span // BS

    def body(place_ref, signal_ref, given_ref, out_ref, held, response_ref, weights, out, sems):
        whole = pltpu.make_async_copy(given_ref, response_ref, sems.at[2 * parts])
        whole.start()
        def load(i):
            return pltpu.make_async_copy(signal_ref.at[:, pl.ds(i * span, span)], held.at[i], sems.at[i])

        def store(i):
            return pltpu.make_async_copy(out.at[i], out_ref.at[i], sems.at[parts + i])

        for i in range(parts):
            load(i).start()
        whole.wait()
        for i in range(parts):

            @pl.when(place_ref[0] == i)
            def _():
                weights[...] = response_ref[:, i * dirs : (i + 1) * dirs]

        for i in range(parts):
            load(i).wait()
            value = jnp.dot(weights[...], held[i], preferred_element_type=F32)
            for b in range(blocks):
                out[i, pl.ds(b, rows, stride=blocks), :] = value[:, b * BS : (b + 1) * BS]
            store(i).start()
        for i in range(parts):
            store(i).wait()

    return pl.pallas_call(
        body,
        in_specs=[SM, HBM, HBM],
        out_specs=HBM,
        out_shape=shape((parts, rows * blocks, BS), F32),
        scratch_shapes=[
            pltpu.VMEM((parts, dirs, span), BF16),
            pltpu.VMEM(response.shape, BF16),
            pltpu.VMEM((rows, dirs), BF16),
            pltpu.VMEM((parts, rows * blocks, BS), F32),
            pltpu.SemaphoreType.DMA((2 * parts + 1,)),
        ],
        compiler_params=params(),
        cost_estimate=cost(2 * rows * dirs * wide, 2 * dirs * wide + 4 * rows * wide),
        name="partial_fit",
    )(place, signal, response)


def set_up(count, index, response, sphere_t, fetched):
    rows, slots = index.shape
    coefs, ns = sphere_t.shape
    room = rows * (slots + 1) + 2 * UNROLL

    def body(count_ref, index_ref, response_ref, sphere_ref, list_ref, steps_ref, g_ref, s_ref, st_ref):
        def row(r, carry):
            def slot(m, inner):
                n_own, n_far = inner
                c = index_ref[r, m]
                near = c < rows
                at = jnp.where(near, n_own, n_far + room)
                list_ref[at] = r + 32 * m + 1024 * jnp.where(near, c, c - rows)
                one = jnp.where(near, 1, 0)
                return n_own + one, n_far + (1 - one)

            n_own, n_far = lax.fori_loop(0, count_ref[r], slot, carry)
            list_ref[n_own] = r + 1024 * rows
            list_ref[n_far + room] = r + 1024 * fetched
            return n_own + (n_own & 1), n_far + (n_far & 1)

        zero = jnp.int32(0)
        n_own, n_far = lax.fori_loop(0, rows, row, (zero, zero))
        for i in range(2 * UNROLL):
            list_ref[n_own + i] = rows + 1024 * rows
            list_ref[n_far + room + i] = rows + 1024 * fetched
        step = 2 * UNROLL
        steps_ref[0] = (n_own + step - 1) // step
        steps_ref[1] = (n_far + step - 1) // step

        def taller(x):
            x = x.astype(F32)
            return jnp.concatenate([x, jnp.zeros((KP - coefs, x.shape[1]), F32)], axis=0)

        low = taller(response_ref[...]).astype(BF16)
        nt = (((1,), (1,)), ((), ()))
        g_ref[...] = lax.dot_general(low, low, nt, preferred_element_type=F32)
        sphere = taller(sphere_ref[...])
        st_ref[...] = sphere.astype(BF16)
        s_ref[...] = sphere.T.astype(BF16)

    return pl.pallas_call(
        body,
        in_specs=[SM, SM, VM, VM],
        out_specs=[SM, SM, VM, VM, VM],
        out_shape=[
            shape((2 * room,), jnp.int32),
            shape((2,), jnp.int32),
            shape((KP, KP), F32),
            shape((ns, KP), BF16),
            shape((KP, ns), BF16),
        ],
        compiler_params=params(),
        cost_estimate=cost(1, 16_000_000),
        name="set_up",
    )(count, index, response, sphere_t)


def send_blocks(want_ref, own, send_ref, sem):
    peers, cap = want_ref.shape
    for p in range(peers):
        for q in range(cap):
            pltpu.make_async_copy(own.at[want_ref[p, q]], send_ref.at[p * cap + q], sem).start()


def wait_all(ref, sem):
    pltpu.make_async_copy(ref, ref, sem).wait()


def first_pack(initial, want):
    rows, wide = initial.shape
    blocks = wide // BS
    peers, cap = want.shape

    def body(want_ref, initial_ref, own_ref, send_ref, order_ref, ends_ref, held, own, sems):
        load = pltpu.make_async_copy(initial_ref, held, sems.at[0])
        load.start()
        load.wait()
        for r in range(blocks):
            block = held[:, r * BS : (r + 1) * BS]
            block = jnp.concatenate([block, jnp.ones((KP - rows, BS), F32)], axis=0)
            own[r] = block.astype(BF16)
        send_blocks(want_ref, own, send_ref, sems.at[1])
        keep = pltpu.make_async_copy(own, own_ref, sems.at[2])
        keep.start()
        for r in range(blocks):
            ends_ref[r] = 0
        for p in range(peers):
            for q in range(cap):
                w = want_ref[p, q]
                ends_ref[w] = ends_ref[w] + 1
        before = jnp.int32(0)
        for r in range(blocks):
            here = ends_ref[r]
            ends_ref[r] = before
            before = before + here
        for p in range(peers):
            for q in range(cap):
                w = want_ref[p, q]
                at = ends_ref[w]
                order_ref[at] = p * cap + q
                ends_ref[w] = at + 1
        wait_all(send_ref, sems.at[1])
        keep.wait()

    return pl.pallas_call(
        body,
        in_specs=[SM, HBM],
        out_specs=[HBM, HBM, SM, SM],
        out_shape=[
            shape((blocks, KP, BS), BF16),
            shape((peers * cap, KP, BS), BF16),
            shape((peers * cap,), jnp.int32),
            shape((blocks,), jnp.int32),
        ],
        scratch_shapes=[
            pltpu.VMEM((rows, wide), F32),
            pltpu.VMEM((blocks, KP, BS), BF16),
            pltpu.SemaphoreType.DMA((3,)),
        ],
        compiler_params=params(),
        cost_estimate=cost(1, 4 * rows * wide + 2 * (blocks + peers * cap) * KP * BS),
        name="first_pack",
    )(want, initial)


def local_terms(pieces, gram, sphere, sphere_t):
    wide = pieces[0].shape[1]
    rows = sum(p.shape[0] for p in pieces)
    ns = sphere.shape[0]
    tile = 512

    def body(*refs):
        ins, (g_ref, s_ref, st_ref), outs = refs[: len(pieces)], refs[len(pieces) :][:3], refs[len(pieces) + 3 :]
        c = jnp.concatenate(
            [r[...] for r in ins] + ([jnp.zeros((KP - rows, tile), F32)] if rows < KP else []), axis=0
        )
        hi = c.astype(BF16)
        lo = (c - hi.astype(F32)).astype(BF16)
        g = g_ref[...]
        gh = g.astype(BF16)
        gl = (g - gh.astype(F32)).astype(BF16)
        fid = jnp.dot(gh, hi, preferred_element_type=F32)
        fid += jnp.dot(gh, lo, preferred_element_type=F32)
        fid += jnp.dot(gl, hi, preferred_element_type=F32)
        amplitude = jnp.dot(s_ref[...], hi, preferred_element_type=F32)
        negative = jnp.minimum(amplitude, 0.0).astype(BF16)
        pulled = jnp.dot(st_ref[...], negative, preferred_element_type=F32)
        value = c - STEP * (fid + SMOOTH * c + PENALTY * pulled)
        at = 0
        for ref, k in zip(outs, CHUNKS):
            ref[...] = value[at : at + k]
            at += k

    def whole(*dims):
        return pl.BlockSpec(dims, lambda i: (0,) * len(dims))

    return pl.pallas_call(
        body,
        grid=(wide // tile,),
        in_specs=[pl.BlockSpec((p.shape[0], tile), lambda i: (0, i)) for p in pieces]
        + [whole(KP, KP), whole(ns, KP), whole(KP, ns)],
        out_specs=[pl.BlockSpec((k, tile), lambda i: (0, i)) for k in CHUNKS],
        out_shape=[shape((k, wide), F32) for k in CHUNKS],
        compiler_params=params(),
        cost_estimate=cost(2 * wide * KP * (3 * KP + 2 * ns), 8 * KP * wide),
        name="local_terms",
    )(*pieces, gram, sphere, sphere_t)


def run_tasks(list_ref, start, steps, blocks_ref, sim_ref, acc_ref, ring, sems, before, loaded, finish_row):
    rows = sim_ref.shape[0]
    nt = (((1,), (1,)), ((), ()))
    wide = 2 * UNROLL

    def fetch(s):
        slot = lax.rem(s, RING)
        for u in range(wide):
            e = list_ref[start + s * wide + u]
            r = jnp.minimum(e & 31, rows - 1)
            to = ring.at[slot * wide + u]
            pltpu.make_async_copy(sim_ref.at[r, (e >> 5) & 31], to, sems.at[slot]).start()

    for s in range(AHEAD):

        @pl.when(s < steps)
        def _():
            fetch(jnp.int32(s))

    before()

    def step(s, done):
        slot = lax.rem(s, RING)

        @pl.when(s + AHEAD < steps)
        def _():
            fetch(s + AHEAD)

        wait_all(ring.at[pl.ds(slot * wide, wide)], sems.at[slot])
        made = []
        for u in range(0, wide, 2):
            e, f = list_ref[start + s * wide + u], list_ref[start + s * wide + u + 1]
            at = slot * wide + u
            left = jnp.concatenate([blocks_ref[e >> 10], blocks_ref[f >> 10]], axis=1)
            right = jnp.concatenate([ring[at], ring[at + 1]], axis=1)
            made.append((e & 31, lax.dot_general(left, right, nt, preferred_element_type=F32)))
        for r, d in made:
            acc_ref[r] = acc_ref[r] + d
        if finish_row is None:
            return done
        pl.when(s == 0)(loaded)
        complete = list_ref[start + (s + 1) * wide] & 31
        lax.fori_loop(done, complete, lambda r, c: finish_row(r), None)
        return complete

    done = lax.fori_loop(0, steps, step, jnp.int32(0))
    if finish_row is None:
        loaded()
        return
    pl.when(steps == 0)(loaded)
    lax.fori_loop(done, rows, lambda r, c: finish_row(r), None)


def graph_call(
    which, tasks, steps, blocks, similarity, extra, finish, out_shape, scratch, sems, name, each_row=None
):
    rows = similarity.shape[0]
    given, k, _ = blocks.shape
    loaded = [x for x in extra if x.dtype != jnp.int32]

    def body(tasks_ref, steps_ref, blocks_ref, sim_ref, *rest):
        extra_refs, rest = rest[: len(extra)], rest[len(extra) :]
        outs, rest = rest[: len(out_shape)], rest[len(out_shape) :]
        held, acc, ring, ring_sems, load_sems, *rest = rest
        buffers, rest = rest[: len(loaded)], rest[len(loaded) :]
        own_scratch, own_sems = rest[: len(scratch)], rest[len(scratch) :]
        first = pltpu.make_async_copy(blocks_ref, held.at[pl.ds(0, given)], load_sems.at[0])
        first.start()
        held[given] = jnp.zeros((k, BS), BF16)
        for r in range(rows + 1):
            acc[r] = jnp.zeros((k, BS), F32)
        loads, ready = [], []
        left = list(buffers)
        for x, ref in zip(extra, extra_refs):
            if x.dtype == jnp.int32:
                ready.append(ref)
                continue
            to = left.pop(0)
            ready.append(to)
            loads.append(pltpu.make_async_copy(ref, to, load_sems.at[len(loads) + 1]))

        def before():
            for load in loads:
                load.start()
            first.wait()

        def all_loaded():
            for load in loads:
                load.wait()

        given_on = (acc, ready, outs, own_scratch, own_sems[0])
        finish_row = None if each_row is None else lambda r: each_row(r, *given_on)
        start = which * (tasks.shape[0] // 2)
        run_tasks(
            tasks_ref, start, steps_ref[which], held, sim_ref, acc, ring, ring_sems, before, all_loaded, finish_row
        )
        finish(*given_on)

    return pl.pallas_call(
        body,
        in_specs=[SM, SM, ANY, HBM] + [SM if x.dtype == jnp.int32 else HBM for x in extra],
        out_specs=[HBM] * len(out_shape),
        out_shape=out_shape,
        scratch_shapes=[
            pltpu.VMEM((given + 1, k, BS), BF16),
            pltpu.VMEM((rows + 1, k, BS), F32),
            pltpu.VMEM((RING * 2 * UNROLL, BS, BS), BF16),
            pltpu.SemaphoreType.DMA((RING,)),
            pltpu.SemaphoreType.DMA((len(loaded) + 1,)),
        ]
        + [pltpu.VMEM(x.shape, x.dtype) for x in loaded]
        + scratch
        + [pltpu.SemaphoreType.DMA((sems,))],
        compiler_params=params(),
        cost_estimate=cost(2 * k * BS * BS * rows * 14, 8_000_000),
        name=name,
    )(tasks, steps, blocks, similarity, *extra)


def first_own(tasks, steps, own, similarity):
    rows = similarity.shape[0]
    k = own.shape[1]

    def finish(acc, extra, outs, scratch, sems):
        out = pltpu.make_async_copy(acc.at[pl.ds(0, rows)], outs[0], sems.at[0])
        out.start()
        out.wait()

    (summed,) = graph_call(
        0, tasks, steps, own, similarity, [], finish, [shape((rows, k, BS), F32)], [], 1, "first_own"
    )
    return summed


def first_far(tasks, steps, recv, similarity, summed, bases):
    rows = similarity.shape[0]
    wide = rows * BS

    def finish(acc, extra, outs, scratch, sems):
        sum_ref, *base_refs = extra
        for r in range(rows):
            at = slice(r * BS, (r + 1) * BS)
            total = acc[r] + sum_ref[r]
            factor = (STEP * SMOOTH) / total[KP - 1 : KP]
            total = total * factor
            low = 0
            for base_ref, to, k in zip(base_refs, scratch, CHUNKS):
                to[:, at] = base_ref[:, at] + total[low : low + k]
                low += k
            scratch[-1][:, at] = jnp.broadcast_to(factor, (8, BS))
        copies = [pltpu.make_async_copy(s, o, sems.at[i]) for i, (s, o) in enumerate(zip(scratch, outs))]
        for copy in copies:
            copy.start()
        for copy in copies:
            copy.wait()

    dims = [(k, wide) for k in CHUNKS] + [(8, wide)]
    *mixed, factor = graph_call(
        1,
        tasks,
        steps,
        recv,
        similarity,
        [summed, *bases],
        finish,
        [shape(d, F32) for d in dims],
        [pltpu.VMEM(d, F32) for d in dims],
        len(dims),
        "first_far",
    )
    return mixed, factor


def next_own(tasks, steps, own, similarity, base, flat, factor):
    rows = similarity.shape[0]
    wide = rows * BS
    k = own.shape[1]

    def finish(acc, extra, outs, scratch, sems):
        base_ref, flat_ref, factor_ref = extra
        real = flat_ref.shape[0] // rows
        for r in range(rows):
            at = slice(r * BS, (r + 1) * BS)
            part = flat_ref[pl.ds(r, real, stride=rows), :]
            part = jnp.concatenate([part, jnp.zeros((k - real, BS), F32)], axis=0)
            scratch[0][:, at] = base_ref[:, at] + STEP * part + acc[r] * factor_ref[0:1, at]
        out = pltpu.make_async_copy(scratch[0], outs[0], sems.at[0])
        out.start()
        out.wait()

    (pre,) = graph_call(
        0,
        tasks,
        steps,
        own,
        similarity,
        [base, flat, factor],
        finish,
        [shape((k, wide), F32)],
        [pltpu.VMEM((k, wide), F32)],
        1,
        "next_own",
    )
    return pre


def hand_on(r, value, order_ref, ends_ref, outs, scratch, sems):
    out_ref, own_ref, send_ref = outs
    out, own = scratch
    out[r] = value
    own[r] = value.astype(BF16)
    at = pl.ds(pl.multiple_of(r * BS, BS), BS)

    def send(j, carry):
        pltpu.make_async_copy(own.at[r], send_ref.at[order_ref[j]], sems.at[0]).start()
        return carry

    lax.fori_loop(jnp.where(r == 0, 0, ends_ref[jnp.maximum(r - 1, 0)]), ends_ref[r], send, 0)
    pltpu.make_async_copy(own.at[r], own_ref.at[r], sems.at[1]).start()
    pltpu.make_async_copy(out.at[r], out_ref.at[:, at], sems.at[2]).start()


def handed(outs, sems):
    out_ref, own_ref, send_ref = outs
    wait_all(send_ref, sems.at[0])
    wait_all(own_ref, sems.at[1])
    wait_all(out_ref, sems.at[2])


def next_far(tasks, steps, recv, similarity, pre, factor, order, ends):
    rows = similarity.shape[0]
    wide = rows * BS
    k = recv.shape[1]

    def each_row(r, acc, extra, outs, scratch, sems):
        pre_ref, factor_ref, order_ref, ends_ref = extra
        at = pl.ds(pl.multiple_of(r * BS, BS), BS)
        value = shrink(pre_ref[:, at] + acc[r] * factor_ref[0:1, at])
        hand_on(r, value, order_ref, ends_ref, outs, scratch, sems)

    def finish(acc, extra, outs, scratch, sems):
        handed(outs, sems)

    return graph_call(
        1,
        tasks,
        steps,
        recv,
        similarity,
        [pre, factor, order, ends],
        finish,
        [shape((k, wide), F32), shape((rows, k, BS), BF16), shape(recv.shape, BF16)],
        [pltpu.VMEM((rows, k, BS), F32), pltpu.VMEM((rows, k, BS), BF16)],
        3,
        "next_far",
        each_row,
    )


def last_far(tasks, steps, recv, similarity, pre, factor, out_rows):
    rows = similarity.shape[0]
    wide = rows * BS

    def each_row(r, acc, extra, outs, scratch, sems):
        pre_ref, factor_ref = extra
        (out,) = scratch
        at = pl.ds(pl.multiple_of(r * BS, BS), BS)
        value = shrink(pre_ref[:, at] + acc[r] * factor_ref[0:1, at])
        out[r] = value[:out_rows]
        pltpu.make_async_copy(out.at[r], outs[0].at[:, at], sems.at[r]).start()

    def finish(acc, extra, outs, scratch, sems):
        for r in range(rows):
            at = slice(r * BS, (r + 1) * BS)
            pltpu.make_async_copy(scratch[0].at[r], outs[0].at[:, at], sems.at[r]).wait()

    (coeffs,) = graph_call(
        1,
        tasks,
        steps,
        recv,
        similarity,
        [pre, factor],
        finish,
        [shape((out_rows, wide), F32)],
        [pltpu.VMEM((rows, out_rows, BS), F32)],
        rows,
        "last_far",
        each_row,
    )
    return coeffs


def finish_first(mixed, flat, order, ends):
    k, wide = mixed.shape
    blocks = wide // BS
    rows = flat.shape[0] // blocks
    fetched = order.shape[0]

    def body(order_ref, ends_ref, mixed_ref, flat_ref, out_ref, own_ref, send_ref, mix, held, out, own, sems):
        loads = [
            pltpu.make_async_copy(mixed_ref, mix, sems.at[3]),
            pltpu.make_async_copy(flat_ref, held, sems.at[4]),
        ]
        for load in loads:
            load.start()
        for load in loads:
            load.wait()
        outs = (out_ref, own_ref, send_ref)

        def each(r, carry):
            at = pl.ds(pl.multiple_of(r * BS, BS), BS)
            part = held[pl.ds(r, rows, stride=blocks), :]
            part = jnp.concatenate([part, jnp.zeros((k - rows, BS), F32)], axis=0)
            value = shrink(mix[:, at] + STEP * part)
            hand_on(r, value, order_ref, ends_ref, outs, (out, own), sems)
            return carry

        lax.fori_loop(0, blocks, each, 0)
        handed(outs, sems)

    return pl.pallas_call(
        body,
        in_specs=[SM, SM, HBM, HBM],
        out_specs=[HBM] * 3,
        out_shape=[
            shape((k, wide), F32),
            shape((blocks, k, BS), BF16),
            shape((fetched, k, BS), BF16),
        ],
        scratch_shapes=[
            pltpu.VMEM((k, wide), F32),
            pltpu.VMEM((rows * blocks, BS), F32),
            pltpu.VMEM((blocks, k, BS), F32),
            pltpu.VMEM((blocks, k, BS), BF16),
            pltpu.SemaphoreType.DMA((5,)),
        ],
        compiler_params=params(),
        cost_estimate=cost(1, 12 * k * wide),
        name="finish_first",
    )(order, ends, mixed, flat)


def local(
    signal,
    response,
    sphere_basis,
    initial,
    similarity,
    neighbour_count,
    neighbour_index,
    fetch_list,
):
    coef_count = initial.shape[0]
    peers = lax.axis_size("vox")
    parts = lax.axis_size("dir")
    dirs = signal.shape[0]

    place = lax.axis_index("dir").reshape(1).astype(jnp.int32)
    partial = partial_fit(place, signal, response, parts)
    flat = lax.psum_scatter(
        partial.reshape(-1, BS), "dir", scatter_dimension=0, tiled=True
    )
    lists, steps, gram, sphere, sphere_t = set_up(
        neighbour_count, neighbour_index, response, sphere_basis.T, fetch_list.size
    )
    want = lax.all_to_all(
        fetch_list.reshape(peers, -1), "vox", split_axis=0, concat_axis=0, tiled=True
    )
    def exchange(send):
        moved = lax.all_to_all(
            send.reshape(peers, -1, BS), "vox", split_axis=0, concat_axis=0, tiled=True
        )
        return moved.reshape(send.shape)

    own, send, order, ends = first_pack(initial, want)
    recv = exchange(send)
    (base,) = local_terms([initial], gram, sphere, sphere_t)
    summed = first_own(lists, steps, own, similarity)
    (mixed,), factor = first_far(lists, steps, recv, similarity, summed, [base])
    coeffs, own, send = finish_first(mixed, flat, order, ends)
    for iteration in range(1, ITERS):
        recv = exchange(send)
        (base,) = local_terms([coeffs], gram, sphere, sphere_t)
        pre = next_own(lists, steps, own, similarity, base, flat, factor)
        if iteration < ITERS - 1:
            coeffs, own, send = next_far(lists, steps, recv, similarity, pre, factor, order, ends)
        else:
            coeffs = last_far(lists, steps, recv, similarity, pre, factor, coef_count)
    return coeffs


def solution(mesh):
    in_specs = (
        P("dir", "vox"),
        P(),
        P(),
        P(None, ("vox", "dir")),
        P(("vox", "dir"), None, None, None),
        P(("vox", "dir")),
        P(("vox", "dir"), None),
        P(("vox", "dir"), None, None),
    )
    out_specs = P(None, ("vox", "dir"))
    return jax.shard_map(local, mesh=mesh, in_specs=in_specs, out_specs=out_specs, check_vma=False)
```

time: 189 us -> 185 us (0.979)
  the two profiles are of different devices: /device:TPU:32 before, /device:TPU:33 now
where the time goes in v2:
time: 185 us; the launch traced here: 184 us
  Pallas kernels  76.2 us (41%)
  waiting for transfers between devices  59 us (32%)
  starting transfers between devices  15.9 us (9%)
  between operations  13.6 us (7%)
  blocking collectives  13 us (7%)
  local copies, waits for them, and re-layouts  6.48 us (4%)
    all_to_all x3, waiting for transfers between devices, exchange(): lax.all_to_all(send.reshape(peers, -1, BS), 'vox', split_axis=0, concat_a...  52.5 us
    pallas_call x6, Pallas kernels, graph_call(): pl.pallas_call(body, in_specs=[SM, SM, ANY, HBM] + [SM if x.dtype == jnp....  41.3 us
    pallas_call x3, Pallas kernels, local_terms(): pl.pallas_call(body, grid=(wide // tile,), in_specs=[pl.BlockSpec((p.shap...  16.3 us
    all_to_all x3, starting transfers between devices, exchange(): lax.all_to_all(send.reshape(peers, -1, BS), 'vox', split_axis=0, concat_a...  15.9 us
    all_to_all x1, blocking collectives, local(): lax.all_to_all(fetch_list.reshape(peers, -1), 'vox', split_axis=0, concat...  13 us
    pallas_call x1, Pallas kernels, partial_fit(): pl.pallas_call(body, in_specs=[SM, HBM, HBM], out_specs=HBM, out_shape=sh...  6.63 us
    reduce_scatter x1, waiting for transfers between devices, local(): lax.psum_scatter(partial.reshape(-1, BS), 'dir', scatter_dimension=0, til...  6.43 us
    unnamed x28, local copies, waits for them, and re-layouts  6.4 us
  transfers between devices with their start and end apart: 4, of which 4 were waited for; matrix products, arithmetic and copies ran while one was open for 0% of the time, Pallas kernels for 25%

profile of v2, /device:TPU:33, one launch (start us, length us, event | category | flops | bytes accessed | tf_op | source)
XLA Modules:
  0.0 184.2 jit_solution(10141011906165866543)
XLA Ops:
  6.5 0.0 reduce-scatter.2.cloned.1.call-start
  6.5 1.0 copy-done.4
  7.5 6.6 %partial_fit.1 = f32[8,2448,128]{2,1,0:T(8,128)} custom-call(s32[1]{0:T(128)} %bitcast.5.place_ref, bf16[150,16384]{1,0:T(8,128)(2,1)} %signal_ref.1, bf16[153,1200]{1,0:T(8,128)(2,1)S(1)} %copy-done.4), custom_call_target="tpu_custom_call" | custom-call | flops 752025600 | bytes 14942208 | tf_op jit(solution)/shard_map/partial_fit/pallas_call | solution.py:76
  14.2 0.0 copy-start.13
  14.2 0.0 copy-start.6
  14.2 0.0 reduce-scatter.2.cloned.1.call-update
  14.2 0.6 copy-done.13
  14.9 0.1 copy.13
  14.9 13.0 %all_to_all.26 = s32[16,1,3]{2,1,0:T(1,128)S(1)} all-to-all(s32[16,1,3]{2,1,0:T(1,128)S(1)} %copy.13), channel_id=1, replica_groups=mesh['vox'=16,'dir'=8] {'vox'}, dimensions={0} | all-to-all | bytes 384 | tf_op jit(solution)/shard_map/all_to_all | solution.py:630
  27.9 0.0 copy-done.6
  27.9 2.8 %first_pack.1 = (bf16[16,160,128]{2,1,0:T(8,128)(2,1)S(1)}, bf16[48,160,128]{2,1,0:T(8,128)(2,1)}, s32[48]{0:T(128)S(1)}, s32[16]{0:T(128)S(1)}) custom-call(s32[16,3]{1,0:T(8,128)S(1)} %bitcast.12, f32[153,2048]{1,0:T(8,128)S(1)} %copy-done.6), custom_call_target="tpu_custom_call" | custom-call | flops 1 | bytes 3874816 | tf_op jit(solution)/shard_map/first_pack/pallas_call | solution.py:199
  30.7 0.0 copy-start.5
  30.7 0.0 copy-start.8
  30.7 0.0 copy-start.9
  30.7 0.0 copy-start.10
  30.7 4.6 %all-to-all-start.1 = ((bf16[16,480,128]{2,1,0:T(8,128)(2,1)}), bf16[16,480,128]{2,1,0:T(8,128)(2,1)}, u32[]{:S(2)}, u32[]{:S(2)}) async-start(bf16[16,480,128]{2,1,0:T(8,128)(2,1)} %bitcast.14), calls=%async_computation.1 | async-start | bytes 3932160 | tf_op jit(solution)/shard_map/all_to_all | solution.py:634
  35.3 0.0 copy-done.5
  35.3 0.0 copy-done.8
  35.3 0.0 copy-done.9
  35.3 0.0 copy-done.10
  35.4 4.5 %set_up.1 = (s32[928]{0:T(1024)S(1)}, s32[2]{0:T(128)S(1)}, f32[160,160]{1,0:T(8,128)S(1)}, bf16[1200,160]{1,0:T(8,128)(2,1)S(1)}, bf16[160,1200]{1,0:T(8,128)(2,1)S(1)}) custom-call(s32[16]{0:T(128)S(1)} %copy-done.10, s32[16,27]{1,0:T(8,128)S(1)} %copy-done.9, bf16[153,1200]{1,0:T(8,128)(2,1)S(1)} %copy-done.5, bf16[153,1200]{1,0:T(8,128)(2,1)S(1)} %bitcast.11), custom_call_target="tpu_custom_call" | custom-call | flops 1 | bytes 16000000 | tf_op jit(solution)/shard_map/set_up/pallas_call | solution.py:135
  39.9 0.0 copy-start.11
  39.9 5.5 %local_terms.3.rest_1_ = f32[160,2048]{1,0:T(8,128)} custom-call(f32[153,2048]{1,0:T(8,128)} %refs_0_.1, f32[160,160]{1,0:T(8,128)S(1)} %get-tuple-element.28.refs_1_, bf16[1200,160]{1,0:T(8,128)(2,1)S(1)} %get-tuple-element.29.refs_2_, bf16[160,1200]{1,0:T(8,128)(2,1)S(1)} %get-tuple-element.30.refs_3_), custom_call_target="tpu_custom_call" | custom-call | flops 1887436800 | bytes 2621440 | tf_op jit(solution)/shard_map/local_terms/pallas_call | solution.py:251
  45.4 0.0 copy-done.11
  45.4 3.5 %first_own.1.rest_0_ = f32[16,160,128]{2,1,0:T(8,128)S(1)} custom-call(s32[928]{0:T(1024)S(1)} %get-tuple-element.22.tasks_ref, s32[2]{0:T(128)S(1)} %get-tuple-element.23.steps_ref, bf16[16,160,128]{2,1,0:T(8,128)(2,1)S(1)} %get-tuple-element.27.blocks_ref, bf16[16,27,128,128]{3,2,1,0:T(8,128)(2,1)} %sim_ref.11), custom_call_target="tpu_custom_call" | custom-call | flops 1174405120 | bytes 8000000 | tf_op jit(solution)/shard_map/first_own/pallas_call | solution.py:362
  48.9 0.0 copy-start.3
  48.9 1.0 copy-done.3
  49.9 10.3 %all-to-all-done.1 = bf16[16,480,128]{2,1,0:T(8,128)(2,1)} async-done(((bf16[16,480,128]{2,1,0:T(8,128)(2,1)}), bf16[16,480,128]{2,1,0:T(8,128)(2,1)}, u32[]{:S(2)}, u32[]{:S(2)}) %all-to-all-start.1) | async-done | bytes 1966112 | tf_op jit(solution)/shard_map/all_to_all | solution.py:634
  60.3 8.1 %first_far.1 = (f32[160,2048]{1,0:T(8,128)S(1)}, f32[8,2048]{1,0:T(8,128)S(1)}) custom-call(s32[928]{0:T(1024)S(1)} %get-tuple-element.22.tasks_ref, s32[2]{0:T(128)S(1)} %get-tuple-element.23.steps_ref, bf16[48,160,128]{2,1,0:T(8,128)(2,1)} %bitcast.4.blocks_ref, bf16[16,27,128,128]{3,2,1,0:T(8,128)(2,1)} %sim_ref.11, f32[16,160,128]{2,1,0:T(8,128)} %copy-done.3, ...), custom_call_target="tpu_custom_call" | custom-call | flops 1174405120 | bytes 8000000 | tf_op jit(solution)/shard_map/first_far/pallas_call | solution.py:362
  68.3 0.0 copy-start.7
  68.4 1.0 copy-done.7
  69.4 6.4 %reduce-scatter.2.cloned.1.call-done.flat_ref.rest_1_ = f32[2448,128]{1,0:T(8,128)} async-done(((f32[19584,128]{1,0:T(8,128)}), f32[2448,128]{1,0:T(8,128)}) %reduce-scatter.2.cloned.1.call-update) | async-done | bytes 1253392 | tf_op jit(solution)/shard_map/reduce_scatter | solution.py:624
  75.8 1.3 copy-done
  77.1 4.7 %finish_first.1 = (f32[160,2048]{1,0:T(8,128)}, bf16[16,160,128]{2,1,0:T(8,128)(2,1)S(1)}, bf16[48,160,128]{2,1,0:T(8,128)(2,1)}) custom-call(s32[48]{0:T(128)S(1)} %get-tuple-element.24.order_ref.rest_2_, s32[16]{0:T(128)S(1)} %get-tuple-element.25.ends_ref.rest_3_, f32[160,2048]{1,0:T(8,128)} %copy-done.7, f32[2448,128]{1,0:T(8,128)S(1)} %copy-done), custom_call_target="tpu_custom_call" | custom-call | flops 1 | bytes 3932160 | tf_op jit(solution)/shard_map/finish_first/pallas_call | solution.py:585
  81.8 0.0 copy-start.12
  81.8 6.7 %all-to-all-start.2 = ((bf16[16,480,128]{2,1,0:T(8,128)(2,1)}), bf16[16,480,128]{2,1,0:T(8,128)(2,1)}, u32[]{:S(2)}, u32[]{:S(2)}) async-start(bf16[16,480,128]{2,1,0:T(8,128)(2,1)} %bitcast.16), calls=%async_computation.3 | async-start | bytes 3932160 | tf_op jit(solution)/shard_map/all_to_all | solution.py:634
  88.6 0.0 copy-done.12
  88.6 0.0 copy-start.1
  88.6 5.5 %local_terms.4.rest_0_ = f32[160,2048]{1,0:T(8,128)} custom-call(f32[160,2048]{1,0:T(8,128)} %get-tuple-element.34.refs_0_, f32[160,160]{1,0:T(8,128)S(1)} %copy-done.12, bf16[1200,160]{1,0:T(8,128)(2,1)S(1)} %get-tuple-element.29.refs_2_, bf16[160,1200]{1,0:T(8,128)(2,1)S(1)} %get-tuple-element.30.refs_3_), custom_call_target="tpu_custom_call" | custom-call | flops 1887436800 | bytes 2621440 | tf_op jit(solution)/shard_map/local_terms/pallas_call | solution.py:251
  94.1 5.2 %next_own.2.rest_0_ = f32[160,2048]{1,0:T(8,128)} custom-call(s32[928]{0:T(1024)S(1)} %get-tuple-element.22.tasks_ref, s32[2]{0:T(128)S(1)} %get-tuple-element.23.steps_ref, bf16[16,160,128]{2,1,0:T(8,128)(2,1)S(1)} %get-tuple-element.33.blocks_ref, bf16[16,27,128,128]{3,2,1,0:T(8,128)(2,1)} %sim_ref.11, f32[160,2048]{1,0:T(8,128)} %local_terms.4.rest_0_, ...), custom_call_target="tpu_custom_call" | custom-call | flops 1174405120 | bytes 8000000 | tf_op jit(solution)/shard_map/next_own/pallas_call | solution.py:362
  99.3 22.0 %all-to-all-done.2 = bf16[16,480,128]{2,1,0:T(8,128)(2,1)} async-done(((bf16[16,480,128]{2,1,0:T(8,128)(2,1)}), bf16[16,480,128]{2,1,0:T(8,128)(2,1)}, u32[]{:S(2)}, u32[]{:S(2)}) %all-to-all-start.2) | async-done | bytes 1966112 | tf_op jit(solution)/shard_map/all_to_all | solution.py:634
  121.3 10.4 %next_far.1 = (f32[160,2048]{1,0:T(8,128)}, bf16[16,160,128]{2,1,0:T(8,128)(2,1)S(1)}, bf16[48,160,128]{2,1,0:T(8,128)(2,1)}) custom-call(s32[928]{0:T(1024)S(1)} %get-tuple-element.22.tasks_ref, s32[2]{0:T(128)S(1)} %get-tuple-element.23.steps_ref, bf16[48,160,128]{2,1,0:T(8,128)(2,1)} %bitcast.8.blocks_ref, bf16[16,27,128,128]{3,2,1,0:T(8,128)(2,1)} %sim_ref.11, ...), custom_call_target="tpu_custom_call" | custom-call | flops 1174405120 | bytes 8000000 | tf_op jit(solution)/shard_map/next_far/pallas_call | solution.py:362
  131.7 4.6 %all-to-all-start.3 = ((bf16[16,480,128]{2,1,0:T(8,128)(2,1)}), bf16[16,480,128]{2,1,0:T(8,128)(2,1)}, u32[]{:S(2)}, u32[]{:S(2)}) async-start(bf16[16,480,128]{2,1,0:T(8,128)(2,1)} %bitcast.15), calls=%async_computation.4 | async-start | bytes 3932160 | tf_op jit(solution)/shard_map/all_to_all | solution.py:634
  136.3 5.4 %local_terms.5.rest_0_ = f32[160,2048]{1,0:T(8,128)} custom-call(f32[160,2048]{1,0:T(8,128)} %get-tuple-element.38.refs_0_, f32[160,160]{1,0:T(8,128)S(1)} %copy-done.12, bf16[1200,160]{1,0:T(8,128)(2,1)S(1)} %get-tuple-element.29.refs_2_, bf16[160,1200]{1,0:T(8,128)(2,1)S(1)} %get-tuple-element.30.refs_3_), custom_call_target="tpu_custom_call" | custom-call | flops 1887436800 | bytes 2621440 | tf_op jit(solution)/shard_map/local_terms/pallas_call | solution.py:251
  141.7 5.2 %next_own.3.rest_0_ = f32[160,2048]{1,0:T(8,128)} custom-call(s32[928]{0:T(1024)S(1)} %get-tuple-element.22.tasks_ref, s32[2]{0:T(128)S(1)} %get-tuple-element.23.steps_ref, bf16[16,160,128]{2,1,0:T(8,128)(2,1)S(1)} %get-tuple-element.37.blocks_ref, bf16[16,27,128,128]{3,2,1,0:T(8,128)(2,1)} %sim_ref.11, f32[160,2048]{1,0:T(8,128)} %local_terms.5.rest_0_, ...), custom_call_target="tpu_custom_call" | custom-call | flops 1174405120 | bytes 8000000 | tf_op jit(solution)/shard_map/next_own/pallas_call | solution.py:362
  146.9 20.2 %all-to-all-done.3 = bf16[16,480,128]{2,1,0:T(8,128)(2,1)} async-done(((bf16[16,480,128]{2,1,0:T(8,128)(2,1)}), bf16[16,480,128]{2,1,0:T(8,128)(2,1)}, u32[]{:S(2)}, u32[]{:S(2)}) %all-to-all-start.3) | async-done | bytes 1966112 | tf_op jit(solution)/shard_map/all_to_all | solution.py:634
  167.1 1.3 copy-done.2
  168.4 9.0 %last_far.1 = f32[153,2048]{1,0:T(8,128)} custom-call(s32[928]{0:T(1024)S(1)} %get-tuple-element.22.tasks_ref, s32[2]{0:T(128)S(1)} %get-tuple-element.23.steps_ref, bf16[48,160,128]{2,1,0:T(8,128)(2,1)} %bitcast.10.blocks_ref, bf16[16,27,128,128]{3,2,1,0:T(8,128)(2,1)} %sim_ref.11, f32[160,2048]{1,0:T(8,128)S(1)} %copy-done.2, ...), custom_call_target="tpu_custom_call" | custom-call | flops 1174405120 | bytes 8000000 | tf_op jit(solution)/shard_map/last_far/pallas_call | solution.py:362
  (4 shorter events, 0.0 us)
Async XLA Ops:
  6.5 69.3 %reduce-scatter.2.cloned.1.call-start = ((), (), s32[]{:S(2)}) async-start(), calls=%async_computation.5 | async-start | bytes 11280384 | tf_op jit(solution)/shard_map/reduce_scatter | solution.py:624
  6.5 1.0 copy-start.4
  14.2 0.7 copy-start.13
  14.2 13.7 %copy-start.6 = (f32[153,2048]{1,0:T(8,128)S(1)}, f32[153,2048]{1,0:T(8,128)}, u32[]{:S(2)}) copy-start(f32[153,2048]{1,0:T(8,128)} %refs_0_.1) | copy-start | bytes 3760132
  30.7 4.6 %copy-start.5 = (bf16[153,1200]{1,0:T(8,128)(2,1)S(1)}, bf16[153,1200]{1,0:T(8,128)(2,1)}, u32[]{:S(2)}) copy-start(bf16[153,1200]{1,0:T(8,128)(2,1)} %given_ref.1) | copy-start | bytes 1101604
  30.7 4.6 %copy-start.8 = (bf16[1200,153]{0,1:T(8,128)(2,1)S(1)}, bf16[1200,153]{0,1:T(8,128)(2,1)}, u32[]{:S(2)}) copy-start(bf16[1200,153]{0,1:T(8,128)(2,1)} %param.10) | copy-start | bytes 1101604
  30.7 4.6 %copy-start.9 = (s32[16,27]{1,0:T(8,128)S(1)}, s32[16,27]{1,0:T(8,128)}, u32[]{:S(2)}) copy-start(s32[16,27]{1,0:T(8,128)} %index_ref.1) | copy-start | bytes 5188
  30.7 4.6 %copy-start.10 = (s32[16]{0:T(128)S(1)}, s32[16]{0:T(128)}, u32[]{:S(2)}) copy-start(s32[16]{0:T(128)} %count_ref.1) | copy-start | bytes 196
  30.7 29.5 %all-to-all-start.1 = ((bf16[16,480,128]{2,1,0:T(8,128)(2,1)}), bf16[16,480,128]{2,1,0:T(8,128)(2,1)}, u32[]{:S(2)}, u32[]{:S(2)}) async-start(bf16[16,480,128]{2,1,0:T(8,128)(2,1)} %bitcast.14), calls=%async_computation.1 | async-start | bytes 3932160 | tf_op jit(solution)/shard_map/all_to_all | solution.py:634
  39.9 5.5 %copy-start.11 = (f32[160,160]{1,0:T(8,128)}, f32[160,160]{1,0:T(8,128)S(1)}, u32[]{:S(2)}) copy-start(f32[160,160]{1,0:T(8,128)S(1)} %get-tuple-element.28.refs_1_) | copy-start | bytes 307204
  48.9 1.1 copy-start.3
  68.3 1.1 copy-start.7
  75.8 1.3 copy-start
  81.8 6.7 %copy-start.12 = (f32[160,160]{1,0:T(8,128)S(1)}, f32[160,160]{1,0:T(8,128)}, u32[]{:S(2)}) copy-start(f32[160,160]{1,0:T(8,128)} %copy-done.11) | copy-start | bytes 307204
  81.8 39.4 %all-to-all-start.2 = ((bf16[16,480,128]{2,1,0:T(8,128)(2,1)}), bf16[16,480,128]{2,1,0:T(8,128)(2,1)}, u32[]{:S(2)}, u32[]{:S(2)}) async-start(bf16[16,480,128]{2,1,0:T(8,128)(2,1)} %bitcast.16), calls=%async_computation.3 | async-start | bytes 3932160 | tf_op jit(solution)/shard_map/all_to_all | solution.py:634
  88.6 5.5 %copy-start.1 = (f32[2448,128]{1,0:T(8,128)S(1)}, f32[2448,128]{1,0:T(8,128)}, u32[]{:S(2)}) copy-start(f32[2448,128]{1,0:T(8,128)} %reduce-scatter.2.cloned.1.call-done.flat_ref.rest_1_) | copy-start | bytes 3760132
  131.7 35.3 %all-to-all-start.3 = ((bf16[16,480,128]{2,1,0:T(8,128)(2,1)}), bf16[16,480,128]{2,1,0:T(8,128)(2,1)}, u32[]{:S(2)}, u32[]{:S(2)}) async-start(bf16[16,480,128]{2,1,0:T(8,128)(2,1)} %bitcast.15), calls=%async_computation.4 | async-start | bytes 3932160 | tf_op jit(solution)/shard_map/all_to_all | solution.py:634
  167.1 1.3 copy-start.2
Sparse Core Ops, SparseCore 0:
  14.3 61.4 reduce-scatter.1

commit v3 on v2

--- a/solution.py
+++ b/solution.py
@@ -40,63 +40,108 @@
     return x - jnp.clip(x, -THRESHOLD, THRESHOLD)
 
 
-def partial_fit(place, signal, response, parts):
+def cut_signal(signal, targets, parts):
     dirs, wide = signal.shape
-    rows = response.shape[0]
     span = wide // parts
-    blocks = span // BS
-
-    def body(place_ref, signal_ref, given_ref, out_ref, held, response_ref, weights, out, sems):
-        whole = pltpu.make_async_copy(given_ref, response_ref, sems.at[2 * parts])
-        whole.start()
+    count = targets.shape[0]
+    pairs = count // 2
+
+    def body(targets_ref, signal_ref, *rest):
+        outs, (held, sems) = rest[:pairs], rest[pairs:]
+
         def load(i):
-            return pltpu.make_async_copy(signal_ref.at[:, pl.ds(i * span, span)], held.at[i], sems.at[i])
+            at = pl.multiple_of(targets_ref[i] * span, span)
+            return pltpu.make_async_copy(signal_ref.at[:, pl.ds(at, span)], held.at[i], sems.at[i])
 
         def store(i):
-            return pltpu.make_async_copy(out.at[i], out_ref.at[i], sems.at[parts + i])
-
-        for i in range(parts):
+            half = pl.ds(i % 2 * span, span)
+            return pltpu.make_async_copy(held.at[i], outs[i // 2].at[:, half], sems.at[count + i])
+
+        for i in range(count):
             load(i).start()
-        whole.wait()
-        for i in range(parts):
-
-            @pl.when(place_ref[0] == i)
-            def _():
-                weights[...] = response_ref[:, i * dirs : (i + 1) * dirs]
-
-        for i in range(parts):
+        for i in range(count):
             load(i).wait()
-            value = jnp.dot(weights[...], held[i], preferred_element_type=F32)
-            for b in range(blocks):
-                out[i, pl.ds(b, rows, stride=blocks), :] = value[:, b * BS : (b + 1) * BS]
             store(i).start()
-        for i in range(parts):
+        for i in range(count):
             store(i).wait()
 
     return pl.pallas_call(
         body,
-        in_specs=[SM, HBM, HBM],
-        out_specs=HBM,
-        out_shape=shape((parts, rows * blocks, BS), F32),
+        in_specs=[SM, HBM],
+        out_specs=[HBM] * pairs,
+        out_shape=[shape((dirs, 2 * span), BF16)] * pairs,
         scratch_shapes=[
-            pltpu.VMEM((parts, dirs, span), BF16),
-            pltpu.VMEM(response.shape, BF16),
-            pltpu.VMEM((rows, dirs), BF16),
-            pltpu.VMEM((parts, rows * blocks, BS), F32),
-            pltpu.SemaphoreType.DMA((2 * parts + 1,)),
+            pltpu.VMEM((count, dirs, span), BF16),
+            pltpu.SemaphoreType.DMA((2 * count,)),
         ],
         compiler_params=params(),
-        cost_estimate=cost(2 * rows * dirs * wide, 2 * dirs * wide + 4 * rows * wide),
-        name="partial_fit",
-    )(place, signal, response)
-
-
-def set_up(count, index, response, sphere_t, fetched):
+        cost_estimate=cost(1, 4 * dirs * wide),
+        name="cut_signal",
+    )(targets, signal)
+
+
+def fit_loads(halves, pieces, refs, buffers, sems):
+    loads = []
+    for i, (x, ref, to) in enumerate(zip(pieces, refs, buffers)):
+        span = to.shape[1]
+        loads.append(pltpu.make_async_copy(ref.at[:, pl.ds(halves[i] * span, span)], to, sems.at[i]))
+    return loads
+
+
+def add_fit(source_ref, weights, pieces, first, at):
+    total = None
+    for i, piece in enumerate(pieces):
+        part = jnp.dot(weights[source_ref[first + i]], piece[:, at], preferred_element_type=F32)
+        total = part if total is None else total + part
+    return total
+
+
+def early_fit(sources, weights, halves, pieces):
+    parts, k, dirs = weights.shape
+    span = pieces[0].shape[1] // 2
+    count = len(pieces)
+    tile = 512
+
+    def body(source_ref, weights_ref, *refs):
+        out_ref, *buffers = refs[count:]
+        out, load_sems, sems = buffers[count:]
+        buffers = buffers[:count]
+        loads = fit_loads(halves, pieces, refs, buffers, load_sems)
+        for load in loads:
+            load.start()
+        for load in loads:
+            load.wait()
+        for c in range(0, span, tile):
+            at = slice(c, c + tile)
+            out[:, at] = add_fit(source_ref, weights_ref, buffers, 0, at)
+        keep = pltpu.make_async_copy(out, out_ref, sems.at[0])
+        keep.start()
+        keep.wait()
+
+    return pl.pallas_call(
+        body,
+        in_specs=[SM, VM] + [HBM] * count,
+        out_specs=HBM,
+        out_shape=shape((k, span), F32),
+        scratch_shapes=[pltpu.VMEM((dirs, span), BF16)] * count
+        + [
+            pltpu.VMEM((k, span), F32),
+            pltpu.SemaphoreType.DMA((count,)),
+            pltpu.SemaphoreType.DMA((1,)),
+        ],
+        compiler_params=params(),
+        cost_estimate=cost(2 * k * dirs * count * span, 2 * dirs * count * span),
+        name="early_fit",
+    )(sources, weights, *pieces)
+
+
+def set_up(count, index, response, sphere_t, parts, fetched):
     rows, slots = index.shape
     coefs, ns = sphere_t.shape
+    dirs = response.shape[1] // parts
     room = rows * (slots + 1) + 2 * UNROLL
 
-    def body(count_ref, index_ref, response_ref, sphere_ref, list_ref, steps_ref, g_ref, s_ref, st_ref):
+    def body(count_ref, index_ref, response_ref, sphere_ref, list_ref, steps_ref, w_ref, g_ref, s_ref, st_ref):
         def row(r, carry):
             def slot(m, inner):
                 n_own, n_far = inner
@@ -125,7 +170,10 @@
             x = x.astype(F32)
             return jnp.concatenate([x, jnp.zeros((KP - coefs, x.shape[1]), F32)], axis=0)
 
-        low = taller(response_ref[...]).astype(BF16)
+        tall = taller(response_ref[...])
+        for i in range(parts):
+            w_ref[i] = tall[:, i * dirs : (i + 1) * dirs].astype(BF16)
+        low = tall.astype(BF16)
         nt = (((1,), (1,)), ((), ()))
         g_ref[...] = lax.dot_general(low, low, nt, preferred_element_type=F32)
         sphere = taller(sphere_ref[...])
@@ -135,10 +183,11 @@
     return pl.pallas_call(
         body,
         in_specs=[SM, SM, VM, VM],
-        out_specs=[SM, SM, VM, VM, VM],
+        out_specs=[SM, SM, VM, VM, VM, VM],
         out_shape=[
             shape((2 * room,), jnp.int32),
             shape((2,), jnp.int32),
+            shape((parts, KP, dirs), BF16),
             shape((KP, KP), F32),
             shape((ns, KP), BF16),
             shape((KP, ns), BF16),
@@ -434,19 +483,16 @@
     return mixed, factor
 
 
-def next_own(tasks, steps, own, similarity, base, flat, factor):
+def next_own(tasks, steps, own, similarity, base, fit, factor):
     rows = similarity.shape[0]
     wide = rows * BS
     k = own.shape[1]
 
     def finish(acc, extra, outs, scratch, sems):
-        base_ref, flat_ref, factor_ref = extra
-        real = flat_ref.shape[0] // rows
+        base_ref, fit_ref, factor_ref = extra
         for r in range(rows):
             at = slice(r * BS, (r + 1) * BS)
-            part = flat_ref[pl.ds(r, real, stride=rows), :]
-            part = jnp.concatenate([part, jnp.zeros((k - real, BS), F32)], axis=0)
-            scratch[0][:, at] = base_ref[:, at] + STEP * part + acc[r] * factor_ref[0:1, at]
+            scratch[0][:, at] = base_ref[:, at] + STEP * fit_ref[:, at] + acc[r] * factor_ref[0:1, at]
         out = pltpu.make_async_copy(scratch[0], outs[0], sems.at[0])
         out.start()
         out.wait()
@@ -457,7 +503,7 @@
         steps,
         own,
         similarity,
-        [base, flat, factor],
+        [base, fit, factor],
         finish,
         [shape((k, wide), F32)],
         [pltpu.VMEM((k, wide), F32)],
@@ -554,54 +600,60 @@
     return coeffs
 
 
-def finish_first(mixed, flat, order, ends):
+def finish_first(mixed, fit, sources, first, weights, halves, pieces, order, ends):
     k, wide = mixed.shape
     blocks = wide // BS
-    rows = flat.shape[0] // blocks
     fetched = order.shape[0]
-
-    def body(order_ref, ends_ref, mixed_ref, flat_ref, out_ref, own_ref, send_ref, mix, held, out, own, sems):
-        loads = [
-            pltpu.make_async_copy(mixed_ref, mix, sems.at[3]),
-            pltpu.make_async_copy(flat_ref, held, sems.at[4]),
-        ]
+    count = len(pieces)
+    dirs = weights.shape[2]
+    group = 4
+
+    def body(order_ref, ends_ref, source_ref, weights_ref, mixed_ref, fit_ref, *refs):
+        out_ref, own_ref, send_ref, fit_out, mix, part, out, own, load_sems, sems, *buffers = refs[count:]
+        loads = fit_loads(halves, pieces, refs, buffers, load_sems)
+        loads.append(pltpu.make_async_copy(mixed_ref, mix, sems.at[3]))
+        loads.append(pltpu.make_async_copy(fit_ref, part, sems.at[4]))
         for load in loads:
             load.start()
         for load in loads:
             load.wait()
         outs = (out_ref, own_ref, send_ref)
-
-        def each(r, carry):
-            at = pl.ds(pl.multiple_of(r * BS, BS), BS)
-            part = held[pl.ds(r, rows, stride=blocks), :]
-            part = jnp.concatenate([part, jnp.zeros((k - rows, BS), F32)], axis=0)
-            value = shrink(mix[:, at] + STEP * part)
-            hand_on(r, value, order_ref, ends_ref, outs, (out, own), sems)
-            return carry
-
-        lax.fori_loop(0, blocks, each, 0)
+        for r in range(0, blocks, group):
+            at = slice(r * BS, (r + group) * BS)
+            total = part[:, at] + add_fit(source_ref, weights_ref, buffers, first, at)
+            part[:, at] = total
+            value = shrink(mix[:, at] + STEP * total)
+            for i in range(group):
+                block = value[:, i * BS : (i + 1) * BS]
+                hand_on(jnp.int32(r + i), block, order_ref, ends_ref, outs, (out, own), sems)
+        keep = pltpu.make_async_copy(part, fit_out, sems.at[5])
+        keep.start()
         handed(outs, sems)
+        keep.wait()
 
     return pl.pallas_call(
         body,
-        in_specs=[SM, SM, HBM, HBM],
-        out_specs=[HBM] * 3,
+        in_specs=[SM, SM, SM, VM, HBM, HBM] + [HBM] * count,
+        out_specs=[HBM] * 4,
         out_shape=[
             shape((k, wide), F32),
             shape((blocks, k, BS), BF16),
             shape((fetched, k, BS), BF16),
+            shape((k, wide), F32),
         ],
         scratch_shapes=[
             pltpu.VMEM((k, wide), F32),
-            pltpu.VMEM((rows * blocks, BS), F32),
+            pltpu.VMEM((k, wide), F32),
             pltpu.VMEM((blocks, k, BS), F32),
             pltpu.VMEM((blocks, k, BS), BF16),
-            pltpu.SemaphoreType.DMA((5,)),
-        ],
+            pltpu.SemaphoreType.DMA((count,)),
+            pltpu.SemaphoreType.DMA((6,)),
+        ]
+        + [pltpu.VMEM((dirs, wide), BF16)] * count,
         compiler_params=params(),
         cost_estimate=cost(1, 12 * k * wide),
         name="finish_first",
-    )(order, ends, mixed, flat)
+    )(order, ends, sources, weights, mixed, fit, *pieces)
 
 
 def local(
@@ -617,15 +669,28 @@
     coef_count = initial.shape[0]
     peers = lax.axis_size("vox")
     parts = lax.axis_size("dir")
-    dirs = signal.shape[0]
-
-    place = lax.axis_index("dir").reshape(1).astype(jnp.int32)
-    partial = partial_fit(place, signal, response, parts)
-    flat = lax.psum_scatter(
-        partial.reshape(-1, BS), "dir", scatter_dimension=0, tiled=True
-    )
-    lists, steps, gram, sphere, sphere_t = set_up(
-        neighbour_count, neighbour_index, response, sphere_basis.T, fetch_list.size
+
+    cores = 2
+    chips = parts // cores
+    me = lax.axis_index("dir").astype(jnp.int32)
+    chip, core = me // cores, me % cores
+    far_chips = (1, chips - 1, *range(2, chips - 1))
+    around = [lax.rem(chip + d, chips) * cores for d in (*far_chips, 0)]
+    targets = jnp.stack([x + y for x in around for y in (core, 1 - core)])
+    *cut, mine = cut_signal(signal, targets, parts)
+    over_z = [
+        lax.ppermute(
+            x, "dir", [(i, (i // cores + d) % chips * cores + i % cores) for i in range(parts)]
+        )
+        for x, d in zip(cut, far_chips)
+    ]
+    swap = [(i, i ^ 1) for i in range(parts)]
+    near_swap = lax.ppermute(mine, "dir", swap)
+    came = [lax.rem(chip + chips - d, chips) * cores for d in (0, *far_chips)]
+    sources = [came[0] + core, came[0] + 1 - core]
+    sources = jnp.stack(sources + [x + core for x in came[1:]] + [x + 1 - core for x in came[1:]])
+    lists, steps, weights, gram, sphere, sphere_t = set_up(
+        neighbour_count, neighbour_index, response, sphere_basis.T, parts, fetch_list.size
     )
     want = lax.all_to_all(
         fetch_list.reshape(peers, -1), "vox", split_axis=0, concat_axis=0, tiled=True
@@ -640,12 +705,18 @@
     recv = exchange(send)
     (base,) = local_terms([initial], gram, sphere, sphere_t)
     summed = first_own(lists, steps, own, similarity)
+    near_z, base, summed = lax.optimization_barrier((over_z[:2], base, summed))
+    swapped = [lax.ppermute(x, "dir", swap) for x in near_z]
+    fit = early_fit(sources, weights, [0, 1, 0, 0], [mine, near_swap, *near_z])
+    far_z, fit = lax.optimization_barrier((over_z[2:], fit))
     (mixed,), factor = first_far(lists, steps, recv, similarity, summed, [base])
-    coeffs, own, send = finish_first(mixed, flat, order, ends)
+    late = [*far_z, *swapped, *(lax.ppermute(x, "dir", swap) for x in far_z)]
+    halves = [0] * len(far_z) + [1] * len(over_z)
+    coeffs, own, send, fit = finish_first(mixed, fit, sources, 4, weights, halves, late, order, ends)
     for iteration in range(1, ITERS):
         recv = exchange(send)
         (base,) = local_terms([coeffs], gram, sphere, sphere_t)
-        pre = next_own(lists, steps, own, similarity, base, flat, factor)
+        pre = next_own(lists, steps, own, similarity, base, fit, factor)
         if iteration < ITERS - 1:
             coeffs, own, send = next_far(lists, steps, recv, similarity, pre, factor, order, ends)
         else:

time: 185 us -> 180 us (0.973)
  the two profiles are of different devices: /device:TPU:33 before, /device:TPU:96 now
where the time goes in v3:
time: 180 us; the launch traced here: 178 us
  Pallas kernels  75.2 us (42%)
  waiting for transfers between devices  61.6 us (34%)
  starting transfers between devices  21 us (12%)
  blocking collectives  14.4 us (8%)
  local copies, waits for them, and re-layouts  5.69 us (3%)
    all_to_all x3, waiting for transfers between devices, exchange(): lax.all_to_all(send.reshape(peers, -1, BS), 'vox', split_axis=0, concat_a...  45.1 us
    pallas_call x6, Pallas kernels, graph_call(): pl.pallas_call(body, in_specs=[SM, SM, ANY, HBM] + [SM if x.dtype == jnp....  36.8 us
    all_to_all x3, starting transfers between devices, exchange(): lax.all_to_all(send.reshape(peers, -1, BS), 'vox', split_axis=0, concat_a...  17.7 us
    ppermute x3, waiting for transfers between devices, local(): lax.ppermute(x, 'dir', [(i, (i // cores + d) % chips * cores + i % cores)...  16.5 us
    pallas_call x3, Pallas kernels, local_terms(): pl.pallas_call(body, grid=(wide // tile,), in_specs=[pl.BlockSpec((p.shap...  16.2 us
    all_to_all x1, blocking collectives, local(): lax.all_to_all(fetch_list.reshape(peers, -1), 'vox', split_axis=0, concat...  14.4 us
    pallas_call x1, Pallas kernels, finish_first(): pl.pallas_call(body, in_specs=[SM, SM, SM, VM, HBM, HBM] + [HBM] * count,...  6.9 us
    unnamed x32, local copies, waits for them, and re-layouts  5.44 us
  transfers between devices with their start and end apart: 10, of which 3 were waited for; matrix products, arithmetic and copies ran while one was open for 0% of the time, Pallas kernels for 27%

profile of v3, /device:TPU:96, one launch (start us, length us, event | category | flops | bytes accessed | tf_op | source)
XLA Modules:
  0.0 178.3 jit_solution(15313350078961838513)
XLA Ops:
  0.0 0.1 stack.62.targets_ref
  0.1 4.1 %cut_signal.1 = (bf16[150,4096]{1,0:T(8,128)(2,1)S(1)}, bf16[150,4096]{1,0:T(8,128)(2,1)}, bf16[150,4096]{1,0:T(8,128)(2,1)}, bf16[150,4096]{1,0:T(8,128)(2,1)}) custom-call(s32[8]{0:T(128)S(1)} %stack.62.targets_ref, bf16[150,16384]{1,0:T(8,128)(2,1)} %signal_ref.1), custom_call_target="tpu_custom_call" | custom-call | flops 1 | bytes 9830400 | tf_op jit(solution)/shard_map/cut_signal/pallas_call | solution.py:68
  4.2 0.1 collective-permute-start
  4.3 2.0 %collective-permute-start.1 = (bf16[150,4096]{1,0:T(8,128)(2,1)}, bf16[150,4096]{1,0:T(8,128)(2,1)}, u32[]{:S(2)}, u32[]{:S(2)}) collective-permute-start(bf16[150,4096]{1,0:T(8,128)(2,1)} %get-tuple-element.41), channel_id=1, source_target_pairs={{0,6},{1,7},{2,0},{3,1},{4,2},{5,3},{6,4},{7,5},{8,14},{9,15},{10,... | collective-permute-start | bytes 3686408 | tf_op jit(solution)/shard_map/ppermute | solution.py:682
  6.3 0.0 collective-permute-start.3
  6.3 0.6 collective-permute-start.2
  6.8 0.1 copy.13
  6.9 14.4 %all_to_all.26 = s32[16,1,3]{2,1,0:T(1,128)S(1)} all-to-all(s32[16,1,3]{2,1,0:T(1,128)S(1)} %copy.13), channel_id=1, replica_groups=mesh['vox'=16,'dir'=8] {'vox'}, dimensions={0} | all-to-all | bytes 384 | tf_op jit(solution)/shard_map/all_to_all | solution.py:695
  21.3 2.7 %first_pack.1 = (bf16[16,160,128]{2,1,0:T(8,128)(2,1)S(1)}, bf16[48,160,128]{2,1,0:T(8,128)(2,1)}, s32[48]{0:T(128)S(1)}, s32[16]{0:T(128)S(1)}) custom-call(s32[16,3]{1,0:T(8,128)S(1)} %bitcast.23, f32[153,2048]{1,0:T(8,128)S(1)} %copy-done.4), custom_call_target="tpu_custom_call" | custom-call | flops 1 | bytes 3874816 | tf_op jit(solution)/shard_map/first_pack/pallas_call | solution.py:248
  24.1 0.0 copy-start.6
  24.1 0.0 copy-start.7
  24.1 0.0 copy-start.8
  24.1 0.0 copy-start.9
  24.1 4.6 %all-to-all-start.1 = ((bf16[16,480,128]{2,1,0:T(8,128)(2,1)}), bf16[16,480,128]{2,1,0:T(8,128)(2,1)}, u32[]{:S(2)}, u32[]{:S(2)}) async-start(bf16[16,480,128]{2,1,0:T(8,128)(2,1)} %bitcast.24), calls=%async_computation.1 | async-start | bytes 3932160 | tf_op jit(solution)/shard_map/all_to_all | solution.py:699
  28.7 4.4 %set_up.1 = (s32[928]{0:T(1024)S(1)}, s32[2]{0:T(128)S(1)}, bf16[8,160,150]{2,1,0:T(8,128)(2,1)}, f32[160,160]{1,0:T(8,128)S(1)}, bf16[1200,160]{1,0:T(8,128)(2,1)S(1)}, /*index=5*/bf16[160,1200]{1,0:T(8,128)(2,1)S(1)}) custom-call(s32[16]{0:T(128)S(1)} %copy-done.9, s32[16,27]{1,0:T(8,128)S(1)} %copy-done.8, bf16[153,1200]{1,0:T(8,128)(2,1)S(1)} %copy-done.6, ...), custom_call_target="tpu_custom_call" | custom-call | flops 1 | bytes 16000000 | tf_op jit(solution)/shard_map/set_up/pallas_call | solution.py:183
  33.2 0.8 copy-done.10
  34.0 0.1 stack.56.source_ref
  34.1 1.1 copy-done.11
  35.2 5.4 %local_terms.3.rest_1_ = f32[160,2048]{1,0:T(8,128)} custom-call(f32[153,2048]{1,0:T(8,128)} %refs_0_.1, f32[160,160]{1,0:T(8,128)S(1)} %get-tuple-element.42.refs_1_, bf16[1200,160]{1,0:T(8,128)(2,1)S(1)} %copy-done.11, bf16[160,1200]{1,0:T(8,128)(2,1)S(1)} %get-tuple-element.44.refs_3_), custom_call_target="tpu_custom_call" | custom-call | flops 1887436800 | bytes 2621440 | tf_op jit(solution)/shard_map/local_terms/pallas_call | solution.py:300
  40.6 3.5 %first_own.1.rest_0_ = f32[16,160,128]{2,1,0:T(8,128)S(1)} custom-call(s32[928]{0:T(1024)S(1)} %get-tuple-element.34.tasks_ref, s32[2]{0:T(128)S(1)} %get-tuple-element.35.steps_ref, bf16[16,160,128]{2,1,0:T(8,128)(2,1)S(1)} %get-tuple-element.45.blocks_ref, bf16[16,27,128,128]{3,2,1,0:T(8,128)(2,1)} %sim_ref.11), custom_call_target="tpu_custom_call" | custom-call | flops 1174405120 | bytes 8000000 | tf_op jit(solution)/shard_map/first_own/pallas_call | solution.py:411
  44.1 0.0 copy-start.1
  44.1 1.0 copy-done.1
  45.1 0.0 collective-permute-done.refs_2_
  45.2 16.5 %collective-permute-done.1.refs_3_ = bf16[150,4096]{1,0:T(8,128)(2,1)} collective-permute-done((bf16[150,4096]{1,0:T(8,128)(2,1)}, bf16[150,4096]{1,0:T(8,128)(2,1)}, u32[]{:S(2)}, u32[]{:S(2)}) %collective-permute-start.1) | collective-permute-done | bytes 1228832 | tf_op jit(solution)/shard_map/ppermute | solution.py:682
  61.7 0.0 collective-permute-start.4
  61.7 0.5 collective-permute-start.5
  62.2 0.0 collective-permute-done.3.refs_1_
  62.2 4.0 %early_fit.1.fit_ref = f32[160,2048]{1,0:T(8,128)} custom-call(s32[8]{0:T(128)S(1)} %stack.56.source_ref, bf16[8,160,150]{2,1,0:T(8,128)(2,1)S(1)} %copy-done.2, bf16[150,4096]{1,0:T(8,128)(2,1)S(1)} %copy-done.5, bf16[150,4096]{1,0:T(8,128)(2,1)} %collective-permute-done.3.refs_1_, bf16[150,4096]{1,0:T(8,128)(2,1)} %collective-permute-done.refs_2_, ...), custom_call_target="tpu_custom_call" | custom-call | flops 393216000 | bytes 2457600 | tf_op jit(solution)/shard_map/early_fit/pallas_call | solution.py:121
  66.2 0.0 collective-permute-done.2.refs_0_
  66.2 0.1 collective-permute-start.6
  66.3 0.0 all-to-all-done.1
  66.3 6.9 %first_far.1 = (f32[160,2048]{1,0:T(8,128)S(1)}, f32[8,2048]{1,0:T(8,128)S(1)}) custom-call(s32[928]{0:T(1024)S(1)} %get-tuple-element.34.tasks_ref, s32[2]{0:T(128)S(1)} %get-tuple-element.35.steps_ref, bf16[48,160,128]{2,1,0:T(8,128)(2,1)} %bitcast.12.blocks_ref, bf16[16,27,128,128]{3,2,1,0:T(8,128)(2,1)} %sim_ref.11, f32[16,160,128]{2,1,0:T(8,128)} %copy-done.1, ...), custom_call_target="tpu_custom_call" | custom-call | flops 1174405120 | bytes 8000000 | tf_op jit(solution)/shard_map/first_far/pallas_call | solution.py:411
  73.2 0.0 copy-start.3
  73.2 1.0 copy-done.3
  74.2 0.0 collective-permute-done.4.refs_1_
  74.2 0.0 collective-permute-done.5.refs_2_
  74.2 6.9 %finish_first.1 = (f32[160,2048]{1,0:T(8,128)}, bf16[16,160,128]{2,1,0:T(8,128)(2,1)S(1)}, bf16[48,160,128]{2,1,0:T(8,128)(2,1)}, f32[160,2048]{1,0:T(8,128)}) custom-call(s32[48]{0:T(128)S(1)} %get-tuple-element.36.order_ref.rest_2_, s32[16]{0:T(128)S(1)} %get-tuple-element.37.ends_ref.rest_3_, s32[8]{0:T(128)S(1)} %stack.56.source_ref, ...), custom_call_target="tpu_custom_call" | custom-call | flops 1 | bytes 3932160 | tf_op jit(solution)/shard_map/finish_first/pallas_call | solution.py:634
  81.2 8.2 %all-to-all-start.2 = ((bf16[16,480,128]{2,1,0:T(8,128)(2,1)}), bf16[16,480,128]{2,1,0:T(8,128)(2,1)}, u32[]{:S(2)}, u32[]{:S(2)}) async-start(bf16[16,480,128]{2,1,0:T(8,128)(2,1)} %bitcast.25), calls=%async_computation.2 | async-start | bytes 3932160 | tf_op jit(solution)/shard_map/all_to_all | solution.py:699
  89.4 5.4 %local_terms.4.rest_0_ = f32[160,2048]{1,0:T(8,128)} custom-call(f32[160,2048]{1,0:T(8,128)} %get-tuple-element.57.refs_0_, f32[160,160]{1,0:T(8,128)S(1)} %get-tuple-element.42.refs_1_, bf16[1200,160]{1,0:T(8,128)(2,1)S(1)} %copy-done.12, bf16[160,1200]{1,0:T(8,128)(2,1)S(1)} %copy-done.14), custom_call_target="tpu_custom_call" | custom-call | flops 1887436800 | bytes 2621440 | tf_op jit(solution)/shard_map/local_terms/pallas_call | solution.py:300
  94.8 4.9 %next_own.2.rest_0_ = f32[160,2048]{1,0:T(8,128)} custom-call(s32[928]{0:T(1024)S(1)} %get-tuple-element.34.tasks_ref, s32[2]{0:T(128)S(1)} %get-tuple-element.35.steps_ref, bf16[16,160,128]{2,1,0:T(8,128)(2,1)S(1)} %get-tuple-element.56.blocks_ref, bf16[16,27,128,128]{3,2,1,0:T(8,128)(2,1)} %sim_ref.11, f32[160,2048]{1,0:T(8,128)} %local_terms.4.rest_0_, ...), custom_call_target="tpu_custom_call" | custom-call | flops 1174405120 | bytes 8000000 | tf_op jit(solution)/shard_map/next_own/pallas_call | solution.py:411
  99.7 22.6 %all-to-all-done.2 = bf16[16,480,128]{2,1,0:T(8,128)(2,1)} async-done(((bf16[16,480,128]{2,1,0:T(8,128)(2,1)}), bf16[16,480,128]{2,1,0:T(8,128)(2,1)}, u32[]{:S(2)}, u32[]{:S(2)}) %all-to-all-start.2) | async-done | bytes 1966112 | tf_op jit(solution)/shard_map/all_to_all | solution.py:699
  122.3 9.2 %next_far.1 = (f32[160,2048]{1,0:T(8,128)}, bf16[16,160,128]{2,1,0:T(8,128)(2,1)S(1)}, bf16[48,160,128]{2,1,0:T(8,128)(2,1)}) custom-call(s32[928]{0:T(1024)S(1)} %get-tuple-element.34.tasks_ref, s32[2]{0:T(128)S(1)} %get-tuple-element.35.steps_ref, bf16[48,160,128]{2,1,0:T(8,128)(2,1)} %bitcast.19.blocks_ref, bf16[16,27,128,128]{3,2,1,0:T(8,128)(2,1)} %sim_ref.11, ...), custom_call_target="tpu_custom_call" | custom-call | flops 1174405120 | bytes 8000000 | tf_op jit(solution)/shard_map/next_far/pallas_call | solution.py:411
  131.5 5.0 %all-to-all-start.3 = ((bf16[16,480,128]{2,1,0:T(8,128)(2,1)}), bf16[16,480,128]{2,1,0:T(8,128)(2,1)}, u32[]{:S(2)}, u32[]{:S(2)}) async-start(bf16[16,480,128]{2,1,0:T(8,128)(2,1)} %bitcast.26), calls=%async_computation.3 | async-start | bytes 3932160 | tf_op jit(solution)/shard_map/all_to_all | solution.py:699
  136.5 5.4 %local_terms.5.rest_0_ = f32[160,2048]{1,0:T(8,128)} custom-call(f32[160,2048]{1,0:T(8,128)} %get-tuple-element.62.refs_0_, f32[160,160]{1,0:T(8,128)S(1)} %get-tuple-element.42.refs_1_, bf16[1200,160]{1,0:T(8,128)(2,1)S(1)} %copy-done.12, bf16[160,1200]{1,0:T(8,128)(2,1)S(1)} %copy-done.14), custom_call_target="tpu_custom_call" | custom-call | flops 1887436800 | bytes 2621440 | tf_op jit(solution)/shard_map/local_terms/pallas_call | solution.py:300
  141.9 4.9 %next_own.3.rest_0_ = f32[160,2048]{1,0:T(8,128)} custom-call(s32[928]{0:T(1024)S(1)} %get-tuple-element.34.tasks_ref, s32[2]{0:T(128)S(1)} %get-tuple-element.35.steps_ref, bf16[16,160,128]{2,1,0:T(8,128)(2,1)S(1)} %get-tuple-element.61.blocks_ref, bf16[16,27,128,128]{3,2,1,0:T(8,128)(2,1)} %sim_ref.11, f32[160,2048]{1,0:T(8,128)} %local_terms.5.rest_0_, ...), custom_call_target="tpu_custom_call" | custom-call | flops 1174405120 | bytes 8000000 | tf_op jit(solution)/shard_map/next_own/pallas_call | solution.py:411
  146.8 22.5 %all-to-all-done.3 = bf16[16,480,128]{2,1,0:T(8,128)(2,1)} async-done(((bf16[16,480,128]{2,1,0:T(8,128)(2,1)}), bf16[16,480,128]{2,1,0:T(8,128)(2,1)}, u32[]{:S(2)}, u32[]{:S(2)}) %all-to-all-start.3) | async-done | bytes 1966112 | tf_op jit(solution)/shard_map/all_to_all | solution.py:699
  169.3 1.3 copy-done
  170.6 7.5 %last_far.1 = f32[153,2048]{1,0:T(8,128)} custom-call(s32[928]{0:T(1024)S(1)} %get-tuple-element.34.tasks_ref, s32[2]{0:T(128)S(1)} %get-tuple-element.35.steps_ref, bf16[48,160,128]{2,1,0:T(8,128)(2,1)} %bitcast.21.blocks_ref, bf16[16,27,128,128]{3,2,1,0:T(8,128)(2,1)} %sim_ref.11, f32[160,2048]{1,0:T(8,128)S(1)} %copy-done, ...), custom_call_target="tpu_custom_call" | custom-call | flops 1174405120 | bytes 8000000 | tf_op jit(solution)/shard_map/last_far/pallas_call | solution.py:411
  (22 shorter events, 0.0 us)
Async XLA Ops:
  0.1 6.8 %copy-start.15 = (s32[1,16,3]{1,0,2:T(1,128)S(1)}, s32[1,16,3]{1,0,2:T(1,128)}, u32[]{:S(2)}) copy-start(s32[1,16,3]{1,0,2:T(1,128)} %param.15) | copy-start | bytes 580
  0.1 21.2 %copy-start.4 = (f32[153,2048]{1,0:T(8,128)S(1)}, f32[153,2048]{1,0:T(8,128)}, u32[]{:S(2)}) copy-start(f32[153,2048]{1,0:T(8,128)} %refs_0_.1) | copy-start | bytes 3760132
  4.2 41.0 %collective-permute-start = (bf16[150,4096]{1,0:T(8,128)(2,1)S(1)}, bf16[150,4096]{1,0:T(8,128)(2,1)}, u32[]{:S(2)}, u32[]{:S(2)}) collective-permute-start(bf16[150,4096]{1,0:T(8,128)(2,1)S(1)} %get-tuple-element.40), channel_id=1, source_target_pairs={{0,2},{1,3},{2,4},{3,5},{4,6},{5,7},{6,0},{7,1},{8,10},{9,11},{10,... | collective-permute-start | bytes 3686408 | tf_op jit(solution)/shard_map/ppermute | solution.py:682
  4.3 57.4 %collective-permute-start.1 = (bf16[150,4096]{1,0:T(8,128)(2,1)}, bf16[150,4096]{1,0:T(8,128)(2,1)}, u32[]{:S(2)}, u32[]{:S(2)}) collective-permute-start(bf16[150,4096]{1,0:T(8,128)(2,1)} %get-tuple-element.41), channel_id=1, source_target_pairs={{0,6},{1,7},{2,0},{3,1},{4,2},{5,3},{6,4},{7,5},{8,14},{9,15},{10,... | collective-permute-start | bytes 3686408 | tf_op jit(solution)/shard_map/ppermute | solution.py:682
  6.3 55.9 %collective-permute-start.3 = (bf16[150,4096]{1,0:T(8,128)(2,1)}, bf16[150,4096]{1,0:T(8,128)(2,1)}, u32[]{:S(2)}, u32[]{:S(2)}) collective-permute-start(bf16[150,4096]{1,0:T(8,128)(2,1)} %get-tuple-element.50.refs_0_), channel_id=1, source_target_pairs={{0,1},{1,0},{2,3},{3,2},{4,5},{5,4},{6,7},{7,6},{8,9},{9,8},{10,11... | collective-permute-start | bytes 3686408 | tf_op jit(solution)/shard_map/ppermute | solution.py:688
  6.3 59.9 %collective-permute-start.2 = (bf16[150,4096]{1,0:T(8,128)(2,1)}, bf16[150,4096]{1,0:T(8,128)(2,1)}, u32[]{:S(2)}, u32[]{:S(2)}) collective-permute-start(bf16[150,4096]{1,0:T(8,128)(2,1)} %get-tuple-element.49), channel_id=1, source_target_pairs={{0,4},{1,5},{2,6},{3,7},{4,0},{5,1},{6,2},{7,3},{8,12},{9,13},{10,... | collective-permute-start | bytes 3686408 | tf_op jit(solution)/shard_map/ppermute | solution.py:682
  24.1 4.6 %copy-start.6 = (bf16[153,1200]{1,0:T(8,128)(2,1)S(1)}, bf16[153,1200]{1,0:T(8,128)(2,1)}, u32[]{:S(2)}) copy-start(bf16[153,1200]{1,0:T(8,128)(2,1)} %response_ref.1) | copy-start | bytes 1101604
  24.1 4.6 %copy-start.7 = (bf16[1200,153]{0,1:T(8,128)(2,1)S(1)}, bf16[1200,153]{0,1:T(8,128)(2,1)}, u32[]{:S(2)}) copy-start(bf16[1200,153]{0,1:T(8,128)(2,1)} %param.10) | copy-start | bytes 1101604
  24.1 4.6 %copy-start.8 = (s32[16,27]{1,0:T(8,128)S(1)}, s32[16,27]{1,0:T(8,128)}, u32[]{:S(2)}) copy-start(s32[16,27]{1,0:T(8,128)} %index_ref.1) | copy-start | bytes 5188
  24.1 4.6 %copy-start.9 = (s32[16]{0:T(128)S(1)}, s32[16]{0:T(128)}, u32[]{:S(2)}) copy-start(s32[16]{0:T(128)} %count_ref.1) | copy-start | bytes 196
  24.1 42.2 %all-to-all-start.1 = ((bf16[16,480,128]{2,1,0:T(8,128)(2,1)}), bf16[16,480,128]{2,1,0:T(8,128)(2,1)}, u32[]{:S(2)}, u32[]{:S(2)}) async-start(bf16[16,480,128]{2,1,0:T(8,128)(2,1)} %bitcast.24), calls=%async_computation.1 | async-start | bytes 3932160 | tf_op jit(solution)/shard_map/all_to_all | solution.py:699
  33.2 0.8 copy-start.10
  34.0 6.6 %copy-start.13 = (bf16[160,1200]{1,0:T(8,128)(2,1)}, bf16[160,1200]{1,0:T(8,128)(2,1)S(1)}, u32[]{:S(2)}) copy-start(bf16[160,1200]{1,0:T(8,128)(2,1)S(1)} %get-tuple-element.44.refs_3_) | copy-start | bytes 1152004
  34.1 1.1 copy-start.11
  40.6 21.6 %copy-start.2 = (bf16[8,160,150]{2,1,0:T(8,128)(2,1)S(1)}, bf16[8,160,150]{2,1,0:T(8,128)(2,1)}, u32[]{:S(2)}) copy-start(bf16[8,160,150]{2,1,0:T(8,128)(2,1)} %get-tuple-element.38.weights_ref) | copy-start | bytes 1152004
  40.6 21.6 %copy-start.5 = (bf16[150,4096]{1,0:T(8,128)(2,1)S(1)}, bf16[150,4096]{1,0:T(8,128)(2,1)}, u32[]{:S(2)}) copy-start(bf16[150,4096]{1,0:T(8,128)(2,1)} %get-tuple-element.50.refs_0_) | copy-start | bytes 3686404
  44.1 1.1 copy-start.1
  61.7 12.6 %collective-permute-start.4 = (bf16[150,4096]{1,0:T(8,128)(2,1)}, bf16[150,4096]{1,0:T(8,128)(2,1)}, u32[]{:S(2)}, u32[]{:S(2)}) collective-permute-start(bf16[150,4096]{1,0:T(8,128)(2,1)} %collective-permute-done.refs_2_), channel_id=1, source_target_pairs={{0,1},{1,0},{2,3},{3,2},{4,5},{5,4},{6,7},{7,6},{8,9},{9,8},{10,11... | collective-permute-start | bytes 3686408 | tf_op jit(solution)/shard_map/ppermute | solution.py:709
  61.7 12.6 %collective-permute-start.5 = (bf16[150,4096]{1,0:T(8,128)(2,1)}, bf16[150,4096]{1,0:T(8,128)(2,1)}, u32[]{:S(2)}, u32[]{:S(2)}) collective-permute-start(bf16[150,4096]{1,0:T(8,128)(2,1)} %collective-permute-done.1.refs_3_), channel_id=1, source_target_pairs={{0,1},{1,0},{2,3},{3,2},{4,5},{5,4},{6,7},{7,6},{8,9},{9,8},{10,11... | collective-permute-start | bytes 3686408 | tf_op jit(solution)/shard_map/ppermute | solution.py:709
  66.2 8.1 %collective-permute-start.6 = (bf16[150,4096]{1,0:T(8,128)(2,1)}, bf16[150,4096]{1,0:T(8,128)(2,1)}, u32[]{:S(2)}, u32[]{:S(2)}) collective-permute-start(bf16[150,4096]{1,0:T(8,128)(2,1)} %collective-permute-done.2.refs_0_), channel_id=1, source_target_pairs={{0,1},{1,0},{2,3},{3,2},{4,5},{5,4},{6,7},{7,6},{8,9},{9,8},{10,11... | collective-permute-start | bytes 3686408 | tf_op jit(solution)/shard_map/ppermute | solution.py:713
  73.2 1.1 copy-start.3
  81.1 8.2 %copy-start.12 = (bf16[1200,160]{1,0:T(8,128)(2,1)S(1)}, bf16[1200,160]{1,0:T(8,128)(2,1)}, u32[]{:S(2)}) copy-start(bf16[1200,160]{1,0:T(8,128)(2,1)} %copy-done.10) | copy-start | bytes 1152004
  81.2 8.2 %copy-start.14 = (bf16[160,1200]{1,0:T(8,128)(2,1)S(1)}, bf16[160,1200]{1,0:T(8,128)(2,1)}, u32[]{:S(2)}) copy-start(bf16[160,1200]{1,0:T(8,128)(2,1)} %copy-done.13) | copy-start | bytes 1152004
  81.2 41.1 %all-to-all-start.2 = ((bf16[16,480,128]{2,1,0:T(8,128)(2,1)}), bf16[16,480,128]{2,1,0:T(8,128)(2,1)}, u32[]{:S(2)}, u32[]{:S(2)}) async-start(bf16[16,480,128]{2,1,0:T(8,128)(2,1)} %bitcast.25), calls=%async_computation.2 | async-start | bytes 3932160 | tf_op jit(solution)/shard_map/all_to_all | solution.py:699
  131.5 37.8 %all-to-all-start.3 = ((bf16[16,480,128]{2,1,0:T(8,128)(2,1)}), bf16[16,480,128]{2,1,0:T(8,128)(2,1)}, u32[]{:S(2)}, u32[]{:S(2)}) async-start(bf16[16,480,128]{2,1,0:T(8,128)(2,1)} %bitcast.26), calls=%async_computation.3 | async-start | bytes 3932160 | tf_op jit(solution)/shard_map/all_to_all | solution.py:699
  169.3 1.3 copy-start

commit v4 on v3

--- a/solution.py
+++ b/solution.py
@@ -24,7 +24,7 @@
 ANY = pl.BlockSpec(memory_space=pl.ANY)
 
 
-def params(mib=52):
+def params(mib=53):
     return pltpu.CompilerParams(vmem_limit_bytes=mib << 20)
 
 

time: 180 us -> 176 us (0.978)
  Pallas kernels: 75.2 us -> 89.8 us
  waiting for transfers between devices: 61.6 us -> 49.1 us
  local copies, waits for them, and re-layouts: 5.69 us -> 0.28 us
    all_to_all x3, waiting for transfers between devices: 45.1 us -> 34.2 us  [exchange(): lax.all_to_all(send.reshape(peers, -1, BS), 'vox', split_axis=0, concat_a...]
    pallas_call x6, Pallas kernels: 36.8 us -> 46.4 us  [graph_call(): pl.pallas_call(body, in_specs=[SM, SM, ANY, HBM] + [SM if x.dtype == jnp....]
    unnamed x32 -> x10, local copies, waits for them, and re-layouts: 5.44 us -> 0.02 us
  transfers between devices with their start and end apart: 10 -> 10, of which waited for: 3 -> 3; matrix products, arithmetic and copies ran while one was open for 0% -> 0% of each run, Pallas kernels for 27% -> 33%
where the time goes in v4:
time: 176 us; the launch traced here: 173 us
  Pallas kernels  89.8 us (51%)
  waiting for transfers between devices  49.1 us (28%)
  starting transfers between devices  19.3 us (11%)
  blocking collectives  14.4 us (8%)
    pallas_call x6, Pallas kernels, graph_call(): pl.pallas_call(body, in_specs=[SM, SM, ANY, HBM] + [SM if x.dtype == jnp....  46.4 us
    all_to_all x3, waiting for transfers between devices, exchange(): lax.all_to_all(send.reshape(peers, -1, BS), 'vox', split_axis=0, concat_a...  34.2 us
    pallas_call x3, Pallas kernels, local_terms(): pl.pallas_call(body, grid=(wide // tile,), in_specs=[pl.BlockSpec((p.shap...  16.9 us
    all_to_all x3, starting transfers between devices, exchange(): lax.all_to_all(send.reshape(peers, -1, BS), 'vox', split_axis=0, concat_a...  16.1 us
    ppermute x3, waiting for transfers between devices, local(): lax.ppermute(x, 'dir', [(i, (i // cores + d) % chips * cores + i % cores)...  14.9 us
    all_to_all x1, blocking collectives, local(): lax.all_to_all(fetch_list.reshape(peers, -1), 'vox', split_axis=0, concat...  14.4 us
    pallas_call x1, Pallas kernels, finish_first(): pl.pallas_call(body, in_specs=[SM, SM, SM, VM, HBM, HBM] + [HBM] * count,...  7.36 us
    pallas_call x1, Pallas kernels, set_up(): pl.pallas_call(body, in_specs=[SM, SM, VM, VM], out_specs=[SM, SM, VM, VM...  6.03 us
  transfers between devices with their start and end apart: 10, of which 3 were waited for; matrix products, arithmetic and copies ran while one was open for 0% of the time, Pallas kernels for 33%

profile of v4, /device:TPU:96, one launch (start us, length us, event | category | flops | bytes accessed | tf_op | source)
XLA Modules:
  0.0 173.2 jit_solution(14765377545970753918)
XLA Ops:
  0.0 0.1 stack.62.targets_ref
  0.1 0.0 copy-start.4
  0.1 5.0 %cut_signal.1 = (bf16[150,4096]{1,0:T(8,128)(2,1)}, bf16[150,4096]{1,0:T(8,128)(2,1)}, bf16[150,4096]{1,0:T(8,128)(2,1)}, bf16[150,4096]{1,0:T(8,128)(2,1)}) custom-call(s32[8]{0:T(128)S(1)} %stack.62.targets_ref, bf16[150,16384]{1,0:T(8,128)(2,1)} %signal_ref.1), custom_call_target="tpu_custom_call" | custom-call | flops 1 | bytes 9830400 | tf_op jit(solution)/shard_map/cut_signal/pallas_call | solution.py:68
  5.1 0.1 collective-permute-start
  5.1 2.0 %collective-permute-start.1 = (bf16[150,4096]{1,0:T(8,128)(2,1)}, bf16[150,4096]{1,0:T(8,128)(2,1)}, u32[]{:S(2)}, u32[]{:S(2)}) collective-permute-start(bf16[150,4096]{1,0:T(8,128)(2,1)} %get-tuple-element.41), channel_id=1, source_target_pairs={{0,6},{1,7},{2,0},{3,1},{4,2},{5,3},{6,4},{7,5},{8,14},{9,15},{10,... | collective-permute-start | bytes 3686408 | tf_op jit(solution)/shard_map/ppermute | solution.py:682
  7.2 0.0 collective-permute-start.3
  7.2 0.6 collective-permute-start.2
  7.7 0.0 copy-done.4
  7.7 0.1 copy.13
  7.8 14.4 %all_to_all.26 = s32[16,1,3]{2,1,0:T(1,128)S(1)} all-to-all(s32[16,1,3]{2,1,0:T(1,128)S(1)} %copy.13), channel_id=1, replica_groups=mesh['vox'=16,'dir'=8] {'vox'}, dimensions={0} | all-to-all | bytes 384 | tf_op jit(solution)/shard_map/all_to_all | solution.py:695
  22.2 3.9 %first_pack.1 = (bf16[16,160,128]{2,1,0:T(8,128)(2,1)S(1)}, bf16[48,160,128]{2,1,0:T(8,128)(2,1)}, s32[48]{0:T(128)S(1)}, s32[16]{0:T(128)S(1)}) custom-call(s32[16,3]{1,0:T(8,128)S(1)} %bitcast.22, f32[153,2048]{1,0:T(8,128)} %refs_0_.1), custom_call_target="tpu_custom_call" | custom-call | flops 1 | bytes 3874816 | tf_op jit(solution)/shard_map/first_pack/pallas_call | solution.py:248
  26.1 0.0 copy-start.1
  26.1 0.0 copy-start.2
  26.2 4.4 %all-to-all-start.1 = ((bf16[16,480,128]{2,1,0:T(8,128)(2,1)}), bf16[16,480,128]{2,1,0:T(8,128)(2,1)}, u32[]{:S(2)}, u32[]{:S(2)}) async-start(bf16[16,480,128]{2,1,0:T(8,128)(2,1)} %bitcast.23), calls=%async_computation.1 | async-start | bytes 3932160 | tf_op jit(solution)/shard_map/all_to_all | solution.py:699
  30.6 0.0 copy-done.1
  30.6 0.0 copy-done.2
  30.6 6.0 %set_up.1 = (s32[928]{0:T(1024)S(1)}, s32[2]{0:T(128)S(1)}, bf16[8,160,150]{2,1,0:T(8,128)(2,1)}, f32[160,160]{1,0:T(8,128)S(1)}, bf16[1200,160]{1,0:T(8,128)(2,1)}, /*index=5*/bf16[160,1200]{1,0:T(8,128)(2,1)S(1)}) custom-call(s32[16]{0:T(128)S(1)} %copy-done.2, s32[16,27]{1,0:T(8,128)S(1)} %copy-done.1, bf16[153,1200]{1,0:T(8,128)(2,1)} %response_ref.1, ...), custom_call_target="tpu_custom_call" | custom-call | flops 1 | bytes 16000000 | tf_op jit(solution)/shard_map/set_up/pallas_call | solution.py:183
  36.7 0.1 stack.56.source_ref
  36.8 5.7 %local_terms.3.rest_1_ = f32[160,2048]{1,0:T(8,128)} custom-call(f32[153,2048]{1,0:T(8,128)} %refs_0_.1, f32[160,160]{1,0:T(8,128)S(1)} %get-tuple-element.42.refs_1_, bf16[1200,160]{1,0:T(8,128)(2,1)} %get-tuple-element.43.refs_2_, bf16[160,1200]{1,0:T(8,128)(2,1)S(1)} %get-tuple-element.44.refs_3_), custom_call_target="tpu_custom_call" | custom-call | flops 1887436800 | bytes 2621440 | tf_op jit(solution)/shard_map/local_terms/pallas_call | solution.py:300
  42.4 0.0 copy-start
  42.4 5.2 %first_own.1.rest_0_ = f32[16,160,128]{2,1,0:T(8,128)} custom-call(s32[928]{0:T(1024)S(1)} %get-tuple-element.34.tasks_ref, s32[2]{0:T(128)S(1)} %get-tuple-element.35.steps_ref, bf16[16,160,128]{2,1,0:T(8,128)(2,1)S(1)} %get-tuple-element.45.blocks_ref, bf16[16,27,128,128]{3,2,1,0:T(8,128)(2,1)} %sim_ref.11), custom_call_target="tpu_custom_call" | custom-call | flops 1174405120 | bytes 8000000 | tf_op jit(solution)/shard_map/first_own/pallas_call | solution.py:411
  47.6 0.0 collective-permute-done.refs_2_
  47.7 14.9 %collective-permute-done.1.refs_3_ = bf16[150,4096]{1,0:T(8,128)(2,1)} collective-permute-done((bf16[150,4096]{1,0:T(8,128)(2,1)}, bf16[150,4096]{1,0:T(8,128)(2,1)}, u32[]{:S(2)}, u32[]{:S(2)}) %collective-permute-start.1) | collective-permute-done | bytes 1228832 | tf_op jit(solution)/shard_map/ppermute | solution.py:682
  62.5 0.0 collective-permute-start.4
  62.5 0.5 collective-permute-start.5
  63.0 0.0 collective-permute-done.3.refs_1_
  63.0 0.0 copy-done
  63.1 4.1 %early_fit.1.fit_ref = f32[160,2048]{1,0:T(8,128)} custom-call(s32[8]{0:T(128)S(1)} %stack.56.source_ref, bf16[8,160,150]{2,1,0:T(8,128)(2,1)S(1)} %copy-done, bf16[150,4096]{1,0:T(8,128)(2,1)} %get-tuple-element.50.refs_0_, bf16[150,4096]{1,0:T(8,128)(2,1)} %collective-permute-done.3.refs_1_, bf16[150,4096]{1,0:T(8,128)(2,1)} %collective-permute-done.refs_2_, ...), custom_call_target="tpu_custom_call" | custom-call | flops 393216000 | bytes 2457600 | tf_op jit(solution)/shard_map/early_fit/pallas_call | solution.py:121
  67.2 0.0 collective-permute-done.2.refs_0_
  67.2 0.0 copy-start.3
  67.2 0.1 collective-permute-start.6
  67.3 0.0 all-to-all-done.1
  67.3 9.3 %first_far.1 = (f32[160,2048]{1,0:T(8,128)}, f32[8,2048]{1,0:T(8,128)S(1)}) custom-call(s32[928]{0:T(1024)S(1)} %get-tuple-element.34.tasks_ref, s32[2]{0:T(128)S(1)} %get-tuple-element.35.steps_ref, bf16[48,160,128]{2,1,0:T(8,128)(2,1)} %bitcast.12.blocks_ref, bf16[16,27,128,128]{3,2,1,0:T(8,128)(2,1)} %sim_ref.11, f32[16,160,128]{2,1,0:T(8,128)} %first_own.1.rest_0_, ...), custom_call_target="tpu_custom_call" | custom-call | flops 1174405120 | bytes 8000000 | tf_op jit(solution)/shard_map/first_far/pallas_call | solution.py:411
  76.6 0.0 copy-done.3
  76.6 0.0 collective-permute-done.4.refs_1_
  76.7 0.0 collective-permute-done.5.refs_2_
  76.7 0.0 collective-permute-done.6.refs_3_
  76.7 7.4 %finish_first.1 = (f32[160,2048]{1,0:T(8,128)}, bf16[16,160,128]{2,1,0:T(8,128)(2,1)S(1)}, bf16[48,160,128]{2,1,0:T(8,128)(2,1)}, f32[160,2048]{1,0:T(8,128)}) custom-call(s32[48]{0:T(128)S(1)} %get-tuple-element.36.order_ref.rest_2_, s32[16]{0:T(128)S(1)} %get-tuple-element.37.ends_ref.rest_3_, s32[8]{0:T(128)S(1)} %stack.56.source_ref, ...), custom_call_target="tpu_custom_call" | custom-call | flops 1 | bytes 3932160 | tf_op jit(solution)/shard_map/finish_first/pallas_call | solution.py:634
  84.0 7.0 %all-to-all-start.2 = ((bf16[16,480,128]{2,1,0:T(8,128)(2,1)}), bf16[16,480,128]{2,1,0:T(8,128)(2,1)}, u32[]{:S(2)}, u32[]{:S(2)}) async-start(bf16[16,480,128]{2,1,0:T(8,128)(2,1)} %bitcast.24), calls=%async_computation.2 | async-start | bytes 3932160 | tf_op jit(solution)/shard_map/all_to_all | solution.py:699
  91.1 5.7 %local_terms.4.rest_0_ = f32[160,2048]{1,0:T(8,128)} custom-call(f32[160,2048]{1,0:T(8,128)} %get-tuple-element.57.refs_0_, f32[160,160]{1,0:T(8,128)S(1)} %get-tuple-element.42.refs_1_, bf16[1200,160]{1,0:T(8,128)(2,1)} %get-tuple-element.43.refs_2_, bf16[160,1200]{1,0:T(8,128)(2,1)S(1)} %get-tuple-element.44.refs_3_), custom_call_target="tpu_custom_call" | custom-call | flops 1887436800 | bytes 2621440 | tf_op jit(solution)/shard_map/local_terms/pallas_call | solution.py:300
  96.8 5.6 %next_own.2.rest_0_ = f32[160,2048]{1,0:T(8,128)} custom-call(s32[928]{0:T(1024)S(1)} %get-tuple-element.34.tasks_ref, s32[2]{0:T(128)S(1)} %get-tuple-element.35.steps_ref, bf16[16,160,128]{2,1,0:T(8,128)(2,1)S(1)} %get-tuple-element.56.blocks_ref, bf16[16,27,128,128]{3,2,1,0:T(8,128)(2,1)} %sim_ref.11, f32[160,2048]{1,0:T(8,128)} %local_terms.4.rest_0_, ...), custom_call_target="tpu_custom_call" | custom-call | flops 1174405120 | bytes 8000000 | tf_op jit(solution)/shard_map/next_own/pallas_call | solution.py:411
  102.3 19.3 %all-to-all-done.2 = bf16[16,480,128]{2,1,0:T(8,128)(2,1)} async-done(((bf16[16,480,128]{2,1,0:T(8,128)(2,1)}), bf16[16,480,128]{2,1,0:T(8,128)(2,1)}, u32[]{:S(2)}, u32[]{:S(2)}) %all-to-all-start.2) | async-done | bytes 1966112 | tf_op jit(solution)/shard_map/all_to_all | solution.py:699
  121.7 11.0 %next_far.1 = (f32[160,2048]{1,0:T(8,128)}, bf16[16,160,128]{2,1,0:T(8,128)(2,1)S(1)}, bf16[48,160,128]{2,1,0:T(8,128)(2,1)}) custom-call(s32[928]{0:T(1024)S(1)} %get-tuple-element.34.tasks_ref, s32[2]{0:T(128)S(1)} %get-tuple-element.35.steps_ref, bf16[48,160,128]{2,1,0:T(8,128)(2,1)} %bitcast.19.blocks_ref, bf16[16,27,128,128]{3,2,1,0:T(8,128)(2,1)} %sim_ref.11, ...), custom_call_target="tpu_custom_call" | custom-call | flops 1174405120 | bytes 8000000 | tf_op jit(solution)/shard_map/next_far/pallas_call | solution.py:411
  132.6 4.6 %all-to-all-start.3 = ((bf16[16,480,128]{2,1,0:T(8,128)(2,1)}), bf16[16,480,128]{2,1,0:T(8,128)(2,1)}, u32[]{:S(2)}, u32[]{:S(2)}) async-start(bf16[16,480,128]{2,1,0:T(8,128)(2,1)} %bitcast.25), calls=%async_computation.3 | async-start | bytes 3932160 | tf_op jit(solution)/shard_map/all_to_all | solution.py:699
  137.2 5.6 %local_terms.5.rest_0_ = f32[160,2048]{1,0:T(8,128)} custom-call(f32[160,2048]{1,0:T(8,128)} %get-tuple-element.62.refs_0_, f32[160,160]{1,0:T(8,128)S(1)} %get-tuple-element.42.refs_1_, bf16[1200,160]{1,0:T(8,128)(2,1)} %get-tuple-element.43.refs_2_, bf16[160,1200]{1,0:T(8,128)(2,1)S(1)} %get-tuple-element.44.refs_3_), custom_call_target="tpu_custom_call" | custom-call | flops 1887436800 | bytes 2621440 | tf_op jit(solution)/shard_map/local_terms/pallas_call | solution.py:300
  142.9 5.6 %next_own.3.rest_0_ = f32[160,2048]{1,0:T(8,128)} custom-call(s32[928]{0:T(1024)S(1)} %get-tuple-element.34.tasks_ref, s32[2]{0:T(128)S(1)} %get-tuple-element.35.steps_ref, bf16[16,160,128]{2,1,0:T(8,128)(2,1)S(1)} %get-tuple-element.61.blocks_ref, bf16[16,27,128,128]{3,2,1,0:T(8,128)(2,1)} %sim_ref.11, f32[160,2048]{1,0:T(8,128)} %local_terms.5.rest_0_, ...), custom_call_target="tpu_custom_call" | custom-call | flops 1174405120 | bytes 8000000 | tf_op jit(solution)/shard_map/next_own/pallas_call | solution.py:411
  148.5 14.8 %all-to-all-done.3 = bf16[16,480,128]{2,1,0:T(8,128)(2,1)} async-done(((bf16[16,480,128]{2,1,0:T(8,128)(2,1)}), bf16[16,480,128]{2,1,0:T(8,128)(2,1)}, u32[]{:S(2)}, u32[]{:S(2)}) %all-to-all-start.3) | async-done | bytes 1966112 | tf_op jit(solution)/shard_map/all_to_all | solution.py:699
  163.3 9.8 %last_far.1 = f32[153,2048]{1,0:T(8,128)} custom-call(s32[928]{0:T(1024)S(1)} %get-tuple-element.34.tasks_ref, s32[2]{0:T(128)S(1)} %get-tuple-element.35.steps_ref, bf16[48,160,128]{2,1,0:T(8,128)(2,1)} %bitcast.21.blocks_ref, bf16[16,27,128,128]{3,2,1,0:T(8,128)(2,1)} %sim_ref.11, f32[160,2048]{1,0:T(8,128)} %next_own.3.rest_0_, ...), custom_call_target="tpu_custom_call" | custom-call | flops 1174405120 | bytes 8000000 | tf_op jit(solution)/shard_map/last_far/pallas_call | solution.py:411
Async XLA Ops:
  0.1 7.6 %copy-start.4 = (s32[1,16,3]{1,0,2:T(1,128)S(1)}, s32[1,16,3]{1,0,2:T(1,128)}, u32[]{:S(2)}) copy-start(s32[1,16,3]{1,0,2:T(1,128)} %param.15) | copy-start | bytes 580
  5.1 42.6 %collective-permute-start = (bf16[150,4096]{1,0:T(8,128)(2,1)}, bf16[150,4096]{1,0:T(8,128)(2,1)}, u32[]{:S(2)}, u32[]{:S(2)}) collective-permute-start(bf16[150,4096]{1,0:T(8,128)(2,1)} %get-tuple-element.40), channel_id=1, source_target_pairs={{0,2},{1,3},{2,4},{3,5},{4,6},{5,7},{6,0},{7,1},{8,10},{9,11},{10,... | collective-permute-start | bytes 3686408 | tf_op jit(solution)/shard_map/ppermute | solution.py:682
  5.1 57.4 %collective-permute-start.1 = (bf16[150,4096]{1,0:T(8,128)(2,1)}, bf16[150,4096]{1,0:T(8,128)(2,1)}, u32[]{:S(2)}, u32[]{:S(2)}) collective-permute-start(bf16[150,4096]{1,0:T(8,128)(2,1)} %get-tuple-element.41), channel_id=1, source_target_pairs={{0,6},{1,7},{2,0},{3,1},{4,2},{5,3},{6,4},{7,5},{8,14},{9,15},{10,... | collective-permute-start | bytes 3686408 | tf_op jit(solution)/shard_map/ppermute | solution.py:682
  7.2 55.9 %collective-permute-start.3 = (bf16[150,4096]{1,0:T(8,128)(2,1)}, bf16[150,4096]{1,0:T(8,128)(2,1)}, u32[]{:S(2)}, u32[]{:S(2)}) collective-permute-start(bf16[150,4096]{1,0:T(8,128)(2,1)} %get-tuple-element.50.refs_0_), channel_id=1, source_target_pairs={{0,1},{1,0},{2,3},{3,2},{4,5},{5,4},{6,7},{7,6},{8,9},{9,8},{10,11... | collective-permute-start | bytes 3686408 | tf_op jit(solution)/shard_map/ppermute | solution.py:688
  7.2 60.1 %collective-permute-start.2 = (bf16[150,4096]{1,0:T(8,128)(2,1)}, bf16[150,4096]{1,0:T(8,128)(2,1)S(1)}, u32[]{:S(2)}, u32[]{:S(2)}) collective-permute-start(bf16[150,4096]{1,0:T(8,128)(2,1)} %get-tuple-element.49), channel_id=1, source_target_pairs={{0,4},{1,5},{2,6},{3,7},{4,0},{5,1},{6,2},{7,3},{8,12},{9,13},{10,... | collective-permute-start | bytes 3686408 | tf_op jit(solution)/shard_map/ppermute | solution.py:682
  26.1 4.5 %copy-start.1 = (s32[16,27]{1,0:T(8,128)S(1)}, s32[16,27]{1,0:T(8,128)}, u32[]{:S(2)}) copy-start(s32[16,27]{1,0:T(8,128)} %index_ref.1) | copy-start | bytes 5188
  26.1 4.5 %copy-start.2 = (s32[16]{0:T(128)S(1)}, s32[16]{0:T(128)}, u32[]{:S(2)}) copy-start(s32[16]{0:T(128)} %count_ref.1) | copy-start | bytes 196
  26.2 41.2 %all-to-all-start.1 = ((bf16[16,480,128]{2,1,0:T(8,128)(2,1)}), bf16[16,480,128]{2,1,0:T(8,128)(2,1)}, u32[]{:S(2)}, u32[]{:S(2)}) async-start(bf16[16,480,128]{2,1,0:T(8,128)(2,1)} %bitcast.23), calls=%async_computation.1 | async-start | bytes 3932160 | tf_op jit(solution)/shard_map/all_to_all | solution.py:699
  42.4 20.6 %copy-start = (bf16[8,160,150]{2,1,0:T(8,128)(2,1)S(1)}, bf16[8,160,150]{2,1,0:T(8,128)(2,1)}, u32[]{:S(2)}) copy-start(bf16[8,160,150]{2,1,0:T(8,128)(2,1)} %get-tuple-element.38.weights_ref) | copy-start | bytes 1152004
  62.5 14.1 %collective-permute-start.4 = (bf16[150,4096]{1,0:T(8,128)(2,1)}, bf16[150,4096]{1,0:T(8,128)(2,1)}, u32[]{:S(2)}, u32[]{:S(2)}) collective-permute-start(bf16[150,4096]{1,0:T(8,128)(2,1)} %collective-permute-done.refs_2_), channel_id=1, source_target_pairs={{0,1},{1,0},{2,3},{3,2},{4,5},{5,4},{6,7},{7,6},{8,9},{9,8},{10,11... | collective-permute-start | bytes 3686408 | tf_op jit(solution)/shard_map/ppermute | solution.py:709
  62.5 14.1 %collective-permute-start.5 = (bf16[150,4096]{1,0:T(8,128)(2,1)}, bf16[150,4096]{1,0:T(8,128)(2,1)}, u32[]{:S(2)}, u32[]{:S(2)}) collective-permute-start(bf16[150,4096]{1,0:T(8,128)(2,1)} %collective-permute-done.1.refs_3_), channel_id=1, source_target_pairs={{0,1},{1,0},{2,3},{3,2},{4,5},{5,4},{6,7},{7,6},{8,9},{9,8},{10,11... | collective-permute-start | bytes 3686408 | tf_op jit(solution)/shard_map/ppermute | solution.py:709
  67.2 9.4 %copy-start.3 = (bf16[150,4096]{1,0:T(8,128)(2,1)}, bf16[150,4096]{1,0:T(8,128)(2,1)S(1)}, u32[]{:S(2)}) copy-start(bf16[150,4096]{1,0:T(8,128)(2,1)S(1)} %collective-permute-done.2.refs_0_) | copy-start | bytes 3686404
  67.2 9.4 %collective-permute-start.6 = (bf16[150,4096]{1,0:T(8,128)(2,1)S(1)}, bf16[150,4096]{1,0:T(8,128)(2,1)}, u32[]{:S(2)}, u32[]{:S(2)}) collective-permute-start(bf16[150,4096]{1,0:T(8,128)(2,1)S(1)} %collective-permute-done.2.refs_0_), channel_id=1, source_target_pairs={{0,1},{1,0},{2,3},{3,2},{4,5},{5,4},{6,7},{7,6},{8,9},{9,8},{10,11... | collective-permute-start | bytes 3686408 | tf_op jit(solution)/shard_map/ppermute | solution.py:713
  84.0 37.6 %all-to-all-start.2 = ((bf16[16,480,128]{2,1,0:T(8,128)(2,1)}), bf16[16,480,128]{2,1,0:T(8,128)(2,1)}, u32[]{:S(2)}, u32[]{:S(2)}) async-start(bf16[16,480,128]{2,1,0:T(8,128)(2,1)} %bitcast.24), calls=%async_computation.2 | async-start | bytes 3932160 | tf_op jit(solution)/shard_map/all_to_all | solution.py:699
  132.6 30.7 %all-to-all-start.3 = ((bf16[16,480,128]{2,1,0:T(8,128)(2,1)}), bf16[16,480,128]{2,1,0:T(8,128)(2,1)}, u32[]{:S(2)}, u32[]{:S(2)}) async-start(bf16[16,480,128]{2,1,0:T(8,128)(2,1)} %bitcast.25), calls=%async_computation.3 | async-start | bytes 3932160 | tf_op jit(solution)/shard_map/all_to_all | solution.py:699
